TPU v7x, 1024 devices: a whole 8x8x8 slice. The times are simulated.
1024 devices in a mesh: mem: 8 (over z), lev: 32 (over y_lo, x), row: 4 (over y_hi, core).
Axes of the slice: x: 8, y: 8 (y_hi: 2, y_lo: 4; y = y_hi * 4 + y_lo), z: 8, core: 2. Of those that a mesh axis runs over, the one named last changes fastest.
Arguments:
- control: bfloat16 [16, 64, 128, 256], P('mem', 'lev', 'row'), may hold values from -6 to 6
- members: bfloat16 [16, 64, 32768], P('mem', None, ('row', 'lev')), may hold values from -3 to 3
- east_coef: float32 [64, 128, 256], P('lev', 'row'), may hold values from 0.12 to 0.245
- south_coef: float32 [64, 128, 256], P('lev', 'row'), may hold values from 0.12 to 0.245
- innovation: float32 [64, 32768], P(None, ('row', 'lev')), may hold values from -6 to 6
- huber_class: int32 [64, 32768], P(None, ('row', 'lev')), may hold values 0 or 1
- band: float32 [7, 64], replicated, may hold values from -0.4 to 0.4
- level_group_index: int32 [64], replicated, may hold values from 0 to 16, never falling along the last dimension, each value on 1 to 8 neighbouring positions
Outputs:
- gradient: float32 [16, 64, 128, 256], P('mem', 'lev', 'row')
Inputs may be any that keep to these rules, and one draw needn't show every extreme that they name: `level_group_index`: never falls along the levels; every group 0 to 16 holds 1 to 8 consecutive levels.
All inputs are finite; a program needn't handle non-finite values. No bound on the sum of `huber_class` on one device may be relied on, other than what follows from the above.
Results may differ from a plain program's by a relative error of at most 0.0003.
Values sent between devices are 32-bit elements; how exact they have to be, the bound alone decides.
A program may use at most 32 MiB of HBM per device.

v0:
```python
import jax
import jax.numpy as jnp
from jax import lax
from jax.sharding import PartitionSpec as P

PASSES = 8


HUBER = 1.0


def from_behind(value, axis, steps):
    count = lax.axis_size(axis)
    initial, last = (max(0, -steps), min(count, count - steps))
    return lax.ppermute(value, axis, [(source, source + steps) for source in range(initial, last)])


def padded(cells, sides, width):
    for axis, dim in sides:
        count = lax.axis_size(axis)
        ends = count - 1
        head = lax.slice_in_dim(cells, 0, width, axis=dim)
        tail = lax.slice_in_dim(cells, cells.shape[dim] - width, cells.shape[dim], axis=dim)
        cells = jnp.concatenate(
            [
                lax.ppermute(tail, axis, [(i, (i + 1) % count) for i in range(ends)]),
                cells,
                lax.ppermute(head, axis, [((i + 1) % count, i) for i in range(ends)]),
            ],
            axis=dim,
        )
    return cells


def smooth_rows(extended, east, south):
    center = extended[..., 1:-1, :]
    flux_x = east * (jnp.roll(center, -1, axis=-1) - center)
    flux_y = south * (extended[..., 1:, :] - extended[..., :-1, :])
    return center + flux_x - jnp.roll(flux_x, 1, axis=-1) + flux_y[..., 1:, :] - flux_y[..., :-1, :]


def vertical_level_matrix(band, level_group_index):
    count = band.shape[1]
    rows = jnp.arange(count)[:, None]
    cols = jnp.arange(count)[None, :]
    same = level_group_index[:, None] == level_group_index[None, :]
    matrix = jnp.zeros((count, count), jnp.float32)
    for offset in range(7):
        coef = band[offset] + (1.0 if offset == 3 else 0.0)
        hit = (cols == rows + offset - 3) & same
        matrix = matrix + jnp.where(hit, coef[:, None], jnp.float32(0.0))
    return matrix


def huber_weight(residual, classes):
    scale = HUBER / jnp.maximum(jnp.abs(residual), HUBER)
    return jnp.where(classes == 1, scale, jnp.float32(1.0)) * residual


def per_device(
    control, members, east_coef, south_coef, innovation, huber_class, band, level_group_index
):
    mem_dev, lev_dev, lat_dev, lon = control.shape
    vertical_matrix = vertical_level_matrix(band, level_group_index)
    next_faces = from_behind(south_coef[:, :1, :], "row", -1)
    south_faces = jnp.concatenate([south_coef, next_faces], axis=1)

    def diffuse(field):
        for step in range(PASSES):
            extended = padded(field, (("row", 2),), 1)
            field = smooth_rows(extended, east_coef, south_faces)
        return field

    smoothed_field = diffuse(control.astype(jnp.float32)).reshape(mem_dev, lev_dev, lat_dev * lon)
    column_stack = lax.all_to_all(smoothed_field, "lev", split_axis=2, concat_axis=1, tiled=True)
    filtered_field = jnp.einsum(
        "zw,fwa->fza", vertical_matrix, column_stack, precision=lax.Precision.HIGHEST
    )
    partial_sum = jnp.sum(members.astype(jnp.float32) * filtered_field, axis=0)
    increment = lax.psum(partial_sum, "mem")
    weighted_field = huber_weight(increment - innovation, huber_class)
    adjoint_field = members.astype(jnp.float32) * weighted_field[None]
    lifted_field = jnp.einsum(
        "fr,tfs->trs", vertical_matrix, adjoint_field, precision=lax.Precision.HIGHEST
    )
    levels = lax.all_to_all(lifted_field, "lev", split_axis=1, concat_axis=2, tiled=True)
    return control.astype(jnp.float32) + diffuse(levels.reshape(mem_dev, lev_dev, lat_dev, lon))


def solution(mesh):
    placed = (
        P("mem", "lev", "row", None),
        P("mem", None, ("row", "lev")),
        P("lev", "row", None),
        P("lev", "row", None),
        P(None, ("row", "lev")),
        P(None, ("row", "lev")),
        P(),
        P(),
    )
    return jax.shard_map(
        per_device,
        mesh=mesh,
        in_specs=placed,
        out_specs=P("mem", "lev", "row", None),
        check_vma=False,
    )
```

profile of v0, /device:TPU:1, one launch (start us, length us, event | category | flops | bytes accessed | tf_op | source)
XLA Modules:
  0.0 382.3 jit_solution(377460291677101628)
XLA Ops:
  7.3 16.1 %collective-permute-start = (f32[2,1,256]{2,1,0:T(1,128)S(1)}, f32[2,1,256]{2,1,0:T(1,128)S(1)}, u32[]{:S(2)}, u32[]{:S(2)}) collective-permute-start(f32[2,1,256]{2,1,0:T(1,128)S(1)} %slice.480), channel_id=1, source_target_pairs={{1,0},{2,1},{3,2},{5,4},{6,5},{7,6},{9,8},{10,9},{11,10},{13,12},{... | collective-permute-start | bytes 6152 | tf_op jit(solution)/shard_map/ppermute | solution.py:15
  24.1 1.9 collective-permute-start.1
  26.0 7.5 %collective-permute-start.2 = (f32[2,2,1,256]{3,2,1,0:T(1,128)S(1)}, f32[2,2,1,256]{3,2,1,0:T(1,128)S(1)}, u32[]{:S(2)}, u32[]{:S(2)}) collective-permute-start(f32[2,2,1,256]{3,2,1,0:T(1,128)S(1)} %get-tuple-element.35), channel_id=1, source_target_pairs={{0,1},{1,2},{2,3},{4,5},{5,6},{6,7},{8,9},{9,10},{10,11},{12,13},{... | collective-permute-start | bytes 12296 | tf_op jit(solution)/shard_map/ppermute | solution.py:26
  35.3 1.0 fusion.19
  38.1 0.9 slice_subtract_fusion.15
  39.2 1.9 collective-permute-start.3
  41.1 7.5 %collective-permute-start.4 = (f32[2,2,1,256]{3,2,1,0:T(1,128)S(1)}, f32[2,2,1,256]{3,2,1,0:T(1,128)S(1)}, u32[]{:S(2)}, u32[]{:S(2)}) collective-permute-start(f32[2,2,1,256]{3,2,1,0:T(1,128)S(1)} %get-tuple-element.33), channel_id=1, source_target_pairs={{0,1},{1,2},{2,3},{4,5},{5,6},{6,7},{8,9},{9,10},{10,11},{12,13},{... | collective-permute-start | bytes 12296 | tf_op jit(solution)/shard_map/ppermute | solution.py:26
  48.7 0.9 fusion.20
  50.0 1.9 collective-permute-start.5
  51.9 7.8 %collective-permute-start.6 = (f32[2,2,1,256]{3,2,1,0:T(1,128)S(1)}, f32[2,2,1,256]{3,2,1,0:T(1,128)S(1)}, u32[]{:S(2)}, u32[]{:S(2)}) collective-permute-start(f32[2,2,1,256]{3,2,1,0:T(1,128)S(1)} %get-tuple-element.31), channel_id=1, source_target_pairs={{0,1},{1,2},{2,3},{4,5},{5,6},{6,7},{8,9},{9,10},{10,11},{12,13},{... | collective-permute-start | bytes 12296 | tf_op jit(solution)/shard_map/ppermute | solution.py:26
  59.7 0.9 fusion.21
  61.0 1.9 collective-permute-start.7
  62.9 7.8 %collective-permute-start.8 = (f32[2,2,1,256]{3,2,1,0:T(1,128)S(1)}, f32[2,2,1,256]{3,2,1,0:T(1,128)S(1)}, u32[]{:S(2)}, u32[]{:S(2)}) collective-permute-start(f32[2,2,1,256]{3,2,1,0:T(1,128)S(1)} %get-tuple-element.29), channel_id=1, source_target_pairs={{0,1},{1,2},{2,3},{4,5},{5,6},{6,7},{8,9},{9,10},{10,11},{12,13},{... | collective-permute-start | bytes 12296 | tf_op jit(solution)/shard_map/ppermute | solution.py:26
  72.0 7.8 %collective-permute-start.10 = (f32[2,2,1,256]{3,2,1,0:T(1,128)S(1)}, f32[2,2,1,256]{3,2,1,0:T(1,128)S(1)}, u32[]{:S(2)}, u32[]{:S(2)}) collective-permute-start(f32[2,2,1,256]{3,2,1,0:T(1,128)S(1)} %get-tuple-element.27), channel_id=1, source_target_pairs={{0,1},{1,2},{2,3},{4,5},{5,6},{6,7},{8,9},{9,10},{10,11},{12,13},{... | collective-permute-start | bytes 12296 | tf_op jit(solution)/shard_map/ppermute | solution.py:26
  79.8 1.9 collective-permute-start.9
  82.0 6.7 %collective-permute-done.9 = f32[2,2,1,256]{3,2,1,0:T(1,128)S(1)} collective-permute-done((f32[2,2,1,256]{3,2,1,0:T(1,128)S(1)}, f32[2,2,1,256]{3,2,1,0:T(1,128)S(1)}, u32[]{:S(2)}, u32[]{:S(2)}) %collective-permute-start.9) | collective-permute-done | bytes 4128 | tf_op jit(solution)/shard_map/ppermute | solution.py:28
  88.9 1.9 collective-permute-start.11
  90.9 7.5 %collective-permute-start.12 = (f32[2,2,1,256]{3,2,1,0:T(1,128)S(1)}, f32[2,2,1,256]{3,2,1,0:T(1,128)S(1)}, u32[]{:S(2)}, u32[]{:S(2)}) collective-permute-start(f32[2,2,1,256]{3,2,1,0:T(1,128)S(1)} %get-tuple-element.25), channel_id=1, source_target_pairs={{0,1},{1,2},{2,3},{4,5},{5,6},{6,7},{8,9},{9,10},{10,11},{12,13},{... | collective-permute-start | bytes 12296 | tf_op jit(solution)/shard_map/ppermute | solution.py:26
  99.4 1.9 collective-permute-start.13
  101.4 8.1 %collective-permute-start.14 = (f32[2,2,1,256]{3,2,1,0:T(1,128)S(1)}, f32[2,2,1,256]{3,2,1,0:T(1,128)S(1)}, u32[]{:S(2)}, u32[]{:S(2)}) collective-permute-start(f32[2,2,1,256]{3,2,1,0:T(1,128)S(1)} %get-tuple-element.23), channel_id=1, source_target_pairs={{0,1},{1,2},{2,3},{4,5},{5,6},{6,7},{8,9},{9,10},{10,11},{12,13},{... | collective-permute-start | bytes 12296 | tf_op jit(solution)/shard_map/ppermute | solution.py:26
  110.5 1.9 collective-permute-start.15
  112.4 8.1 %collective-permute-start.16 = (f32[2,2,1,256]{3,2,1,0:T(1,128)S(1)}, f32[2,2,1,256]{3,2,1,0:T(1,128)S(1)}, u32[]{:S(2)}, u32[]{:S(2)}) collective-permute-start(f32[2,2,1,256]{3,2,1,0:T(1,128)S(1)} %get-tuple-element.21), channel_id=1, source_target_pairs={{0,1},{1,2},{2,3},{4,5},{5,6},{6,7},{8,9},{9,10},{10,11},{12,13},{... | collective-permute-start | bytes 12296 | tf_op jit(solution)/shard_map/ppermute | solution.py:26
  121.4 5.9 %copy.11 = f32[2,2,32,256]{1,0,3,2:T(2,128)} copy(f32[2,2,32,256]{3,2,1,0:T(8,128)S(1)} %slice_subtract_fusion.8) | data formatting | bytes 262144 | tf_op jit(solution)/shard_map/sub | solution.py:39
  127.3 14.0 %reshape.67 = f32[32,1,1024]{2,1,0:T(1,128)} reshape(f32[8192,2,2]{2,1,0:T(2,128)} %bitcast.58) | data formatting | bytes 262144
  141.3 3.9 %all-to-all-start = ((f32[32,1,1024]{2,1,0:T(1,128)}), f32[32,1,1024]{2,1,0:T(1,128)S(1)}, u32[]{:S(2)}, u32[]{:S(2)}) async-start(f32[32,1,1024]{2,1,0:T(1,128)} %reshape.67), calls=%async_computation | async-start | bytes 262144 | tf_op jit(solution)/shard_map/all_to_all | solution.py:75
  145.3 9.3 %all-to-all-done = f32[32,1,1024]{2,1,0:T(1,128)S(1)} async-done(((f32[32,1,1024]{2,1,0:T(1,128)}), f32[32,1,1024]{2,1,0:T(1,128)S(1)}, u32[]{:S(2)}, u32[]{:S(2)}) %all-to-all-start) | async-done | bytes 131104 | tf_op jit(solution)/shard_map/all_to_all | solution.py:75
  155.1 0.9 reduce
  156.1 14.2 %reshape.68 = f32[8192,2,2]{2,1,0:T(2,128)} reshape(f32[32,1024]{1,0:T(8,128)S(1)} %reduce) | data formatting | bytes 262144
  170.3 9.6 %copy.12 = f32[2,2,32,256]{3,1,2,0:T(2,128)S(1)} copy(f32[2,2,32,256]{1,0,3,2:T(2,128)} %bitcast.59) | data formatting | bytes 262144 | tf_op jit(solution)/shard_map/all_to_all | solution.py:75
  180.0 1.0 fusion.1
  181.1 81.8 %all-reduce.2.cloned.1.call-done = f32[64,256]{1,0:T(8,128)} async-done(((f32[64,256]{1,0:T(8,128)}), f32[64,256]{1,0:T(8,128)}) %all-reduce.2.cloned.1.call-update) | async-done | bytes 65552 | tf_op jit(solution)/shard_map/psum | solution.py:80
  264.2 18.8 %all_to_all.33 = f32[2,64,256]{2,0,1:T(2,128)S(1)} all-to-all(f32[2,64,256]{2,0,1:T(2,128)S(1)} %copy.14), channel_id=1, replica_groups=mesh['mem'=8,'lev'=32,'row'=4] {'lev'}, dimensions={1} | all-to-all | bytes 262144 | tf_op jit(solution)/shard_map/all_to_all | solution.py:86
  283.2 9.1 %collective-permute-start.17 = (f32[2,2,1,256]{3,2,1,0:T(1,128)S(1)}, f32[2,2,1,256]{3,2,1,0:T(1,128)S(1)}, u32[]{:S(2)}, u32[]{:S(2)}) collective-permute-start(f32[2,2,1,256]{3,2,1,0:T(1,128)S(1)} %get-tuple-element.20), channel_id=1, source_target_pairs={{1,0},{2,1},{3,2},{5,4},{6,5},{7,6},{9,8},{10,9},{11,10},{13,12},{... | collective-permute-start | bytes 12296 | tf_op jit(solution)/shard_map/ppermute | solution.py:28
  292.3 4.4 %collective-permute-start.18 = (f32[2,2,1,256]{3,2,1,0:T(1,128)S(1)}, f32[2,2,1,256]{3,2,1,0:T(1,128)S(1)}, u32[]{:S(2)}, u32[]{:S(2)}) collective-permute-start(f32[2,2,1,256]{3,2,1,0:T(1,128)S(1)} %get-tuple-element.19), channel_id=1, source_target_pairs={{0,1},{1,2},{2,3},{4,5},{5,6},{6,7},{8,9},{9,10},{10,11},{12,13},{... | collective-permute-start | bytes 12296 | tf_op jit(solution)/shard_map/ppermute | solution.py:26
  297.7 1.9 collective-permute-start.19
  299.6 8.1 %collective-permute-start.20 = (f32[2,2,1,256]{3,2,1,0:T(1,128)S(1)}, f32[2,2,1,256]{3,2,1,0:T(1,128)S(1)}, u32[]{:S(2)}, u32[]{:S(2)}) collective-permute-start(f32[2,2,1,256]{3,2,1,0:T(1,128)S(1)} %get-tuple-element.17), channel_id=1, source_target_pairs={{0,1},{1,2},{2,3},{4,5},{5,6},{6,7},{8,9},{9,10},{10,11},{12,13},{... | collective-permute-start | bytes 12296 | tf_op jit(solution)/shard_map/ppermute | solution.py:26
  308.7 1.9 collective-permute-start.21
  310.7 8.1 %collective-permute-start.22 = (f32[2,2,1,256]{3,2,1,0:T(1,128)S(1)}, f32[2,2,1,256]{3,2,1,0:T(1,128)S(1)}, u32[]{:S(2)}, u32[]{:S(2)}) collective-permute-start(f32[2,2,1,256]{3,2,1,0:T(1,128)S(1)} %get-tuple-element.15), channel_id=1, source_target_pairs={{0,1},{1,2},{2,3},{4,5},{5,6},{6,7},{8,9},{9,10},{10,11},{12,13},{... | collective-permute-start | bytes 12296 | tf_op jit(solution)/shard_map/ppermute | solution.py:26
  319.8 1.9 collective-permute-start.23
  321.7 8.1 %collective-permute-start.24 = (f32[2,2,1,256]{3,2,1,0:T(1,128)S(1)}, f32[2,2,1,256]{3,2,1,0:T(1,128)S(1)}, u32[]{:S(2)}, u32[]{:S(2)}) collective-permute-start(f32[2,2,1,256]{3,2,1,0:T(1,128)S(1)} %get-tuple-element.13), channel_id=1, source_target_pairs={{0,1},{1,2},{2,3},{4,5},{5,6},{6,7},{8,9},{9,10},{10,11},{12,13},{... | collective-permute-start | bytes 12296 | tf_op jit(solution)/shard_map/ppermute | solution.py:26
  330.8 1.9 collective-permute-start.25
  332.7 8.1 %collective-permute-start.26 = (f32[2,2,1,256]{3,2,1,0:T(1,128)S(1)}, f32[2,2,1,256]{3,2,1,0:T(1,128)S(1)}, u32[]{:S(2)}, u32[]{:S(2)}) collective-permute-start(f32[2,2,1,256]{3,2,1,0:T(1,128)S(1)} %get-tuple-element.11), channel_id=1, source_target_pairs={{0,1},{1,2},{2,3},{4,5},{5,6},{6,7},{8,9},{9,10},{10,11},{12,13},{... | collective-permute-start | bytes 12296 | tf_op jit(solution)/shard_map/ppermute | solution.py:26
  341.8 1.9 collective-permute-start.27
  343.8 8.1 %collective-permute-start.28 = (f32[2,2,1,256]{3,2,1,0:T(1,128)S(1)}, f32[2,2,1,256]{3,2,1,0:T(1,128)S(1)}, u32[]{:S(2)}, u32[]{:S(2)}) collective-permute-start(f32[2,2,1,256]{3,2,1,0:T(1,128)S(1)} %get-tuple-element.9), channel_id=1, source_target_pairs={{0,1},{1,2},{2,3},{4,5},{5,6},{6,7},{8,9},{9,10},{10,11},{12,13},{... | collective-permute-start | bytes 12296 | tf_op jit(solution)/shard_map/ppermute | solution.py:26
  352.9 1.9 collective-permute-start.29
  354.8 8.1 %collective-permute-start.30 = (f32[2,2,1,256]{3,2,1,0:T(1,128)S(1)}, f32[2,2,1,256]{3,2,1,0:T(1,128)S(1)}, u32[]{:S(2)}, u32[]{:S(2)}) collective-permute-start(f32[2,2,1,256]{3,2,1,0:T(1,128)S(1)} %get-tuple-element.7), channel_id=1, source_target_pairs={{0,1},{1,2},{2,3},{4,5},{5,6},{6,7},{8,9},{9,10},{10,11},{12,13},{... | collective-permute-start | bytes 12296 | tf_op jit(solution)/shard_map/ppermute | solution.py:26
  363.9 1.9 collective-permute-start.31
  365.8 8.1 %collective-permute-start.32 = (f32[2,2,1,256]{3,2,1,0:T(1,128)S(1)}, f32[2,2,1,256]{3,2,1,0:T(1,128)S(1)}, u32[]{:S(2)}, u32[]{:S(2)}) collective-permute-start(f32[2,2,1,256]{3,2,1,0:T(1,128)S(1)} %get-tuple-element.5), channel_id=1, source_target_pairs={{0,1},{1,2},{2,3},{4,5},{5,6},{6,7},{8,9},{9,10},{10,11},{12,13},{... | collective-permute-start | bytes 12296 | tf_op jit(solution)/shard_map/ppermute | solution.py:26
  (169 shorter events, 20.7 us)
Async XLA Ops:
  6.5 75.2 %copy-start = (f32[2,32,256]{2,1,0:T(8,128)S(1)}, f32[2,32,256]{2,1,0:T(8,128)}, u32[]{:S(2)}) copy-start(f32[2,32,256]{2,1,0:T(8,128)} %param.10) | copy-start | bytes 196612
  7.3 29.9 %collective-permute-start = (f32[2,1,256]{2,1,0:T(1,128)S(1)}, f32[2,1,256]{2,1,0:T(1,128)S(1)}, u32[]{:S(2)}, u32[]{:S(2)}) collective-permute-start(f32[2,1,256]{2,1,0:T(1,128)S(1)} %slice.480), channel_id=1, source_target_pairs={{1,0},{2,1},{3,2},{5,4},{6,5},{7,6},{9,8},{10,9},{11,10},{13,12},{... | collective-permute-start | bytes 6152 | tf_op jit(solution)/shard_map/ppermute | solution.py:15
  24.1 13.9 %collective-permute-start.1 = (f32[2,2,1,256]{3,2,1,0:T(1,128)S(1)}, f32[2,2,1,256]{3,2,1,0:T(1,128)S(1)}, u32[]{:S(2)}, u32[]{:S(2)}) collective-permute-start(f32[2,2,1,256]{3,2,1,0:T(1,128)S(1)} %get-tuple-element.36), channel_id=1, source_target_pairs={{1,0},{2,1},{3,2},{5,4},{6,5},{7,6},{9,8},{10,9},{11,10},{13,12},{... | collective-permute-start | bytes 12296 | tf_op jit(solution)/shard_map/ppermute | solution.py:28
  26.0 12.0 %collective-permute-start.2 = (f32[2,2,1,256]{3,2,1,0:T(1,128)S(1)}, f32[2,2,1,256]{3,2,1,0:T(1,128)S(1)}, u32[]{:S(2)}, u32[]{:S(2)}) collective-permute-start(f32[2,2,1,256]{3,2,1,0:T(1,128)S(1)} %get-tuple-element.35), channel_id=1, source_target_pairs={{0,1},{1,2},{2,3},{4,5},{5,6},{6,7},{8,9},{9,10},{10,11},{12,13},{... | collective-permute-start | bytes 12296 | tf_op jit(solution)/shard_map/ppermute | solution.py:26
  39.2 10.5 %collective-permute-start.3 = (f32[2,2,1,256]{3,2,1,0:T(1,128)S(1)}, f32[2,2,1,256]{3,2,1,0:T(1,128)S(1)}, u32[]{:S(2)}, u32[]{:S(2)}) collective-permute-start(f32[2,2,1,256]{3,2,1,0:T(1,128)S(1)} %get-tuple-element.34), channel_id=1, source_target_pairs={{1,0},{2,1},{3,2},{5,4},{6,5},{7,6},{9,8},{10,9},{11,10},{13,12},{... | collective-permute-start | bytes 12296 | tf_op jit(solution)/shard_map/ppermute | solution.py:28
  41.1 8.6 %collective-permute-start.4 = (f32[2,2,1,256]{3,2,1,0:T(1,128)S(1)}, f32[2,2,1,256]{3,2,1,0:T(1,128)S(1)}, u32[]{:S(2)}, u32[]{:S(2)}) collective-permute-start(f32[2,2,1,256]{3,2,1,0:T(1,128)S(1)} %get-tuple-element.33), channel_id=1, source_target_pairs={{0,1},{1,2},{2,3},{4,5},{5,6},{6,7},{8,9},{9,10},{10,11},{12,13},{... | collective-permute-start | bytes 12296 | tf_op jit(solution)/shard_map/ppermute | solution.py:26
  50.0 10.7 %collective-permute-start.5 = (f32[2,2,1,256]{3,2,1,0:T(1,128)S(1)}, f32[2,2,1,256]{3,2,1,0:T(1,128)S(1)}, u32[]{:S(2)}, u32[]{:S(2)}) collective-permute-start(f32[2,2,1,256]{3,2,1,0:T(1,128)S(1)} %get-tuple-element.32), channel_id=1, source_target_pairs={{1,0},{2,1},{3,2},{5,4},{6,5},{7,6},{9,8},{10,9},{11,10},{13,12},{... | collective-permute-start | bytes 12296 | tf_op jit(solution)/shard_map/ppermute | solution.py:28
  51.9 8.8 %collective-permute-start.6 = (f32[2,2,1,256]{3,2,1,0:T(1,128)S(1)}, f32[2,2,1,256]{3,2,1,0:T(1,128)S(1)}, u32[]{:S(2)}, u32[]{:S(2)}) collective-permute-start(f32[2,2,1,256]{3,2,1,0:T(1,128)S(1)} %get-tuple-element.31), channel_id=1, source_target_pairs={{0,1},{1,2},{2,3},{4,5},{5,6},{6,7},{8,9},{9,10},{10,11},{12,13},{... | collective-permute-start | bytes 12296 | tf_op jit(solution)/shard_map/ppermute | solution.py:26
  61.0 10.7 %collective-permute-start.7 = (f32[2,2,1,256]{3,2,1,0:T(1,128)S(1)}, f32[2,2,1,256]{3,2,1,0:T(1,128)S(1)}, u32[]{:S(2)}, u32[]{:S(2)}) collective-permute-start(f32[2,2,1,256]{3,2,1,0:T(1,128)S(1)} %get-tuple-element.30), channel_id=1, source_target_pairs={{1,0},{2,1},{3,2},{5,4},{6,5},{7,6},{9,8},{10,9},{11,10},{13,12},{... | collective-permute-start | bytes 12296 | tf_op jit(solution)/shard_map/ppermute | solution.py:28
  62.9 8.8 %collective-permute-start.8 = (f32[2,2,1,256]{3,2,1,0:T(1,128)S(1)}, f32[2,2,1,256]{3,2,1,0:T(1,128)S(1)}, u32[]{:S(2)}, u32[]{:S(2)}) collective-permute-start(f32[2,2,1,256]{3,2,1,0:T(1,128)S(1)} %get-tuple-element.29), channel_id=1, source_target_pairs={{0,1},{1,2},{2,3},{4,5},{5,6},{6,7},{8,9},{9,10},{10,11},{12,13},{... | collective-permute-start | bytes 12296 | tf_op jit(solution)/shard_map/ppermute | solution.py:26
  72.0 9.9 %collective-permute-start.10 = (f32[2,2,1,256]{3,2,1,0:T(1,128)S(1)}, f32[2,2,1,256]{3,2,1,0:T(1,128)S(1)}, u32[]{:S(2)}, u32[]{:S(2)}) collective-permute-start(f32[2,2,1,256]{3,2,1,0:T(1,128)S(1)} %get-tuple-element.27), channel_id=1, source_target_pairs={{0,1},{1,2},{2,3},{4,5},{5,6},{6,7},{8,9},{9,10},{10,11},{12,13},{... | collective-permute-start | bytes 12296 | tf_op jit(solution)/shard_map/ppermute | solution.py:26
  79.8 8.8 %collective-permute-start.9 = (f32[2,2,1,256]{3,2,1,0:T(1,128)S(1)}, f32[2,2,1,256]{3,2,1,0:T(1,128)S(1)}, u32[]{:S(2)}, u32[]{:S(2)}) collective-permute-start(f32[2,2,1,256]{3,2,1,0:T(1,128)S(1)} %get-tuple-element.28), channel_id=1, source_target_pairs={{1,0},{2,1},{3,2},{5,4},{6,5},{7,6},{9,8},{10,9},{11,10},{13,12},{... | collective-permute-start | bytes 12296 | tf_op jit(solution)/shard_map/ppermute | solution.py:28
  88.9 9.7 %collective-permute-start.11 = (f32[2,2,1,256]{3,2,1,0:T(1,128)S(1)}, f32[2,2,1,256]{3,2,1,0:T(1,128)S(1)}, u32[]{:S(2)}, u32[]{:S(2)}) collective-permute-start(f32[2,2,1,256]{3,2,1,0:T(1,128)S(1)} %get-tuple-element.26), channel_id=1, source_target_pairs={{1,0},{2,1},{3,2},{5,4},{6,5},{7,6},{9,8},{10,9},{11,10},{13,12},{... | collective-permute-start | bytes 12296 | tf_op jit(solution)/shard_map/ppermute | solution.py:28
  90.9 8.3 %collective-permute-start.12 = (f32[2,2,1,256]{3,2,1,0:T(1,128)S(1)}, f32[2,2,1,256]{3,2,1,0:T(1,128)S(1)}, u32[]{:S(2)}, u32[]{:S(2)}) collective-permute-start(f32[2,2,1,256]{3,2,1,0:T(1,128)S(1)} %get-tuple-element.25), channel_id=1, source_target_pairs={{0,1},{1,2},{2,3},{4,5},{5,6},{6,7},{8,9},{9,10},{10,11},{12,13},{... | collective-permute-start | bytes 12296 | tf_op jit(solution)/shard_map/ppermute | solution.py:26
  99.4 10.2 %collective-permute-start.13 = (f32[2,2,1,256]{3,2,1,0:T(1,128)S(1)}, f32[2,2,1,256]{3,2,1,0:T(1,128)S(1)}, u32[]{:S(2)}, u32[]{:S(2)}) collective-permute-start(f32[2,2,1,256]{3,2,1,0:T(1,128)S(1)} %get-tuple-element.24), channel_id=1, source_target_pairs={{1,0},{2,1},{3,2},{5,4},{6,5},{7,6},{9,8},{10,9},{11,10},{13,12},{... | collective-permute-start | bytes 12296 | tf_op jit(solution)/shard_map/ppermute | solution.py:28
  101.4 8.8 %collective-permute-start.14 = (f32[2,2,1,256]{3,2,1,0:T(1,128)S(1)}, f32[2,2,1,256]{3,2,1,0:T(1,128)S(1)}, u32[]{:S(2)}, u32[]{:S(2)}) collective-permute-start(f32[2,2,1,256]{3,2,1,0:T(1,128)S(1)} %get-tuple-element.23), channel_id=1, source_target_pairs={{0,1},{1,2},{2,3},{4,5},{5,6},{6,7},{8,9},{9,10},{10,11},{12,13},{... | collective-permute-start | bytes 12296 | tf_op jit(solution)/shard_map/ppermute | solution.py:26
  110.5 10.2 %collective-permute-start.15 = (f32[2,2,1,256]{3,2,1,0:T(1,128)S(1)}, f32[2,2,1,256]{3,2,1,0:T(1,128)S(1)}, u32[]{:S(2)}, u32[]{:S(2)}) collective-permute-start(f32[2,2,1,256]{3,2,1,0:T(1,128)S(1)} %get-tuple-element.22), channel_id=1, source_target_pairs={{1,0},{2,1},{3,2},{5,4},{6,5},{7,6},{9,8},{10,9},{11,10},{13,12},{... | collective-permute-start | bytes 12296 | tf_op jit(solution)/shard_map/ppermute | solution.py:28
  112.4 8.8 %collective-permute-start.16 = (f32[2,2,1,256]{3,2,1,0:T(1,128)S(1)}, f32[2,2,1,256]{3,2,1,0:T(1,128)S(1)}, u32[]{:S(2)}, u32[]{:S(2)}) collective-permute-start(f32[2,2,1,256]{3,2,1,0:T(1,128)S(1)} %get-tuple-element.21), channel_id=1, source_target_pairs={{0,1},{1,2},{2,3},{4,5},{5,6},{6,7},{8,9},{9,10},{10,11},{12,13},{... | collective-permute-start | bytes 12296 | tf_op jit(solution)/shard_map/ppermute | solution.py:26
  121.4 23.9 %copy-start.4 = (f32[7,64]{1,0:T(8,128)S(1)}, f32[7,64]{1,0:T(8,128)}, u32[]{:S(2)}) copy-start(f32[7,64]{1,0:T(8,128)} %param.14) | copy-start | bytes 5380
  141.3 13.2 %all-to-all-start = ((f32[32,1,1024]{2,1,0:T(1,128)}), f32[32,1,1024]{2,1,0:T(1,128)S(1)}, u32[]{:S(2)}, u32[]{:S(2)}) async-start(f32[32,1,1024]{2,1,0:T(1,128)} %reshape.67), calls=%async_computation | async-start | bytes 262144 | tf_op jit(solution)/shard_map/all_to_all | solution.py:75
  145.2 117.7 %all-reduce.2.cloned.1.call-start = ((), (), s32[]{:S(2)}) async-start(), calls=%async_computation.2 | async-start | bytes 131072 | tf_op jit(solution)/shard_map/psum | solution.py:80
  156.0 24.0 %copy-start.5 = (bf16[2,64,256]{2,1,0:T(8,128)(2,1)S(1)}, bf16[2,64,256]{2,1,0:T(8,128)(2,1)}, u32[]{:S(2)}) copy-start(bf16[2,64,256]{2,1,0:T(8,128)(2,1)} %param.9) | copy-start | bytes 196612
  156.1 24.0 %copy-start.6 = (s32[64]{0:T(128)S(1)}, s32[64]{0:T(128)}, u32[]{:S(2)}) copy-start(s32[64]{0:T(128)} %param.15) | copy-start | bytes 772
  156.1 106.8 %copy-start.2 = (f32[64,256]{1,0:T(8,128)S(1)}, f32[64,256]{1,0:T(8,128)}, u32[]{:S(2)}) copy-start(f32[64,256]{1,0:T(8,128)} %param.12) | copy-start | bytes 196612
  156.1 106.8 %copy-start.3 = (s32[64,256]{1,0:T(8,128)S(1)}, s32[64,256]{1,0:T(8,128)}, u32[]{:S(2)}) copy-start(s32[64,256]{1,0:T(8,128)} %param.13) | copy-start | bytes 196612
  283.2 13.7 %collective-permute-start.17 = (f32[2,2,1,256]{3,2,1,0:T(1,128)S(1)}, f32[2,2,1,256]{3,2,1,0:T(1,128)S(1)}, u32[]{:S(2)}, u32[]{:S(2)}) collective-permute-start(f32[2,2,1,256]{3,2,1,0:T(1,128)S(1)} %get-tuple-element.20), channel_id=1, source_target_pairs={{1,0},{2,1},{3,2},{5,4},{6,5},{7,6},{9,8},{10,9},{11,10},{13,12},{... | collective-permute-start | bytes 12296 | tf_op jit(solution)/shard_map/ppermute | solution.py:28
  292.3 5.1 %collective-permute-start.18 = (f32[2,2,1,256]{3,2,1,0:T(1,128)S(1)}, f32[2,2,1,256]{3,2,1,0:T(1,128)S(1)}, u32[]{:S(2)}, u32[]{:S(2)}) collective-permute-start(f32[2,2,1,256]{3,2,1,0:T(1,128)S(1)} %get-tuple-element.19), channel_id=1, source_target_pairs={{0,1},{1,2},{2,3},{4,5},{5,6},{6,7},{8,9},{9,10},{10,11},{12,13},{... | collective-permute-start | bytes 12296 | tf_op jit(solution)/shard_map/ppermute | solution.py:26
  296.8 77.9 %copy-start.1 = (bf16[2,2,32,256]{3,2,1,0:T(8,128)(2,1)S(1)}, bf16[2,2,32,256]{3,2,1,0:T(8,128)(2,1)}, u32[]{:S(2)}) copy-start(bf16[2,2,32,256]{3,2,1,0:T(8,128)(2,1)} %param.8) | copy-start | bytes 196612
  297.7 10.2 %collective-permute-start.19 = (f32[2,2,1,256]{3,2,1,0:T(1,128)S(1)}, f32[2,2,1,256]{3,2,1,0:T(1,128)S(1)}, u32[]{:S(2)}, u32[]{:S(2)}) collective-permute-start(f32[2,2,1,256]{3,2,1,0:T(1,128)S(1)} %get-tuple-element.18), channel_id=1, source_target_pairs={{1,0},{2,1},{3,2},{5,4},{6,5},{7,6},{9,8},{10,9},{11,10},{13,12},{... | collective-permute-start | bytes 12296 | tf_op jit(solution)/shard_map/ppermute | solution.py:28
  299.6 8.8 %collective-permute-start.20 = (f32[2,2,1,256]{3,2,1,0:T(1,128)S(1)}, f32[2,2,1,256]{3,2,1,0:T(1,128)S(1)}, u32[]{:S(2)}, u32[]{:S(2)}) collective-permute-start(f32[2,2,1,256]{3,2,1,0:T(1,128)S(1)} %get-tuple-element.17), channel_id=1, source_target_pairs={{0,1},{1,2},{2,3},{4,5},{5,6},{6,7},{8,9},{9,10},{10,11},{12,13},{... | collective-permute-start | bytes 12296 | tf_op jit(solution)/shard_map/ppermute | solution.py:26
  308.7 10.2 %collective-permute-start.21 = (f32[2,2,1,256]{3,2,1,0:T(1,128)S(1)}, f32[2,2,1,256]{3,2,1,0:T(1,128)S(1)}, u32[]{:S(2)}, u32[]{:S(2)}) collective-permute-start(f32[2,2,1,256]{3,2,1,0:T(1,128)S(1)} %get-tuple-element.16), channel_id=1, source_target_pairs={{1,0},{2,1},{3,2},{5,4},{6,5},{7,6},{9,8},{10,9},{11,10},{13,12},{... | collective-permute-start | bytes 12296 | tf_op jit(solution)/shard_map/ppermute | solution.py:28
  310.7 8.8 %collective-permute-start.22 = (f32[2,2,1,256]{3,2,1,0:T(1,128)S(1)}, f32[2,2,1,256]{3,2,1,0:T(1,128)S(1)}, u32[]{:S(2)}, u32[]{:S(2)}) collective-permute-start(f32[2,2,1,256]{3,2,1,0:T(1,128)S(1)} %get-tuple-element.15), channel_id=1, source_target_pairs={{0,1},{1,2},{2,3},{4,5},{5,6},{6,7},{8,9},{9,10},{10,11},{12,13},{... | collective-permute-start | bytes 12296 | tf_op jit(solution)/shard_map/ppermute | solution.py:26
  319.8 10.2 %collective-permute-start.23 = (f32[2,2,1,256]{3,2,1,0:T(1,128)S(1)}, f32[2,2,1,256]{3,2,1,0:T(1,128)S(1)}, u32[]{:S(2)}, u32[]{:S(2)}) collective-permute-start(f32[2,2,1,256]{3,2,1,0:T(1,128)S(1)} %get-tuple-element.14), channel_id=1, source_target_pairs={{1,0},{2,1},{3,2},{5,4},{6,5},{7,6},{9,8},{10,9},{11,10},{13,12},{... | collective-permute-start | bytes 12296 | tf_op jit(solution)/shard_map/ppermute | solution.py:28
  321.7 8.8 %collective-permute-start.24 = (f32[2,2,1,256]{3,2,1,0:T(1,128)S(1)}, f32[2,2,1,256]{3,2,1,0:T(1,128)S(1)}, u32[]{:S(2)}, u32[]{:S(2)}) collective-permute-start(f32[2,2,1,256]{3,2,1,0:T(1,128)S(1)} %get-tuple-element.13), channel_id=1, source_target_pairs={{0,1},{1,2},{2,3},{4,5},{5,6},{6,7},{8,9},{9,10},{10,11},{12,13},{... | collective-permute-start | bytes 12296 | tf_op jit(solution)/shard_map/ppermute | solution.py:26
  330.8 10.2 %collective-permute-start.25 = (f32[2,2,1,256]{3,2,1,0:T(1,128)S(1)}, f32[2,2,1,256]{3,2,1,0:T(1,128)S(1)}, u32[]{:S(2)}, u32[]{:S(2)}) collective-permute-start(f32[2,2,1,256]{3,2,1,0:T(1,128)S(1)} %get-tuple-element.12), channel_id=1, source_target_pairs={{1,0},{2,1},{3,2},{5,4},{6,5},{7,6},{9,8},{10,9},{11,10},{13,12},{... | collective-permute-start | bytes 12296 | tf_op jit(solution)/shard_map/ppermute | solution.py:28
  332.7 8.8 %collective-permute-start.26 = (f32[2,2,1,256]{3,2,1,0:T(1,128)S(1)}, f32[2,2,1,256]{3,2,1,0:T(1,128)S(1)}, u32[]{:S(2)}, u32[]{:S(2)}) collective-permute-start(f32[2,2,1,256]{3,2,1,0:T(1,128)S(1)} %get-tuple-element.11), channel_id=1, source_target_pairs={{0,1},{1,2},{2,3},{4,5},{5,6},{6,7},{8,9},{9,10},{10,11},{12,13},{... | collective-permute-start | bytes 12296 | tf_op jit(solution)/shard_map/ppermute | solution.py:26
  341.8 10.2 %collective-permute-start.27 = (f32[2,2,1,256]{3,2,1,0:T(1,128)S(1)}, f32[2,2,1,256]{3,2,1,0:T(1,128)S(1)}, u32[]{:S(2)}, u32[]{:S(2)}) collective-permute-start(f32[2,2,1,256]{3,2,1,0:T(1,128)S(1)} %get-tuple-element.10), channel_id=1, source_target_pairs={{1,0},{2,1},{3,2},{5,4},{6,5},{7,6},{9,8},{10,9},{11,10},{13,12},{... | collective-permute-start | bytes 12296 | tf_op jit(solution)/shard_map/ppermute | solution.py:28
  343.8 8.8 %collective-permute-start.28 = (f32[2,2,1,256]{3,2,1,0:T(1,128)S(1)}, f32[2,2,1,256]{3,2,1,0:T(1,128)S(1)}, u32[]{:S(2)}, u32[]{:S(2)}) collective-permute-start(f32[2,2,1,256]{3,2,1,0:T(1,128)S(1)} %get-tuple-element.9), channel_id=1, source_target_pairs={{0,1},{1,2},{2,3},{4,5},{5,6},{6,7},{8,9},{9,10},{10,11},{12,13},{... | collective-permute-start | bytes 12296 | tf_op jit(solution)/shard_map/ppermute | solution.py:26
  352.9 10.2 %collective-permute-start.29 = (f32[2,2,1,256]{3,2,1,0:T(1,128)S(1)}, f32[2,2,1,256]{3,2,1,0:T(1,128)S(1)}, u32[]{:S(2)}, u32[]{:S(2)}) collective-permute-start(f32[2,2,1,256]{3,2,1,0:T(1,128)S(1)} %get-tuple-element.8), channel_id=1, source_target_pairs={{1,0},{2,1},{3,2},{5,4},{6,5},{7,6},{9,8},{10,9},{11,10},{13,12},{... | collective-permute-start | bytes 12296 | tf_op jit(solution)/shard_map/ppermute | solution.py:28
  354.8 8.8 %collective-permute-start.30 = (f32[2,2,1,256]{3,2,1,0:T(1,128)S(1)}, f32[2,2,1,256]{3,2,1,0:T(1,128)S(1)}, u32[]{:S(2)}, u32[]{:S(2)}) collective-permute-start(f32[2,2,1,256]{3,2,1,0:T(1,128)S(1)} %get-tuple-element.7), channel_id=1, source_target_pairs={{0,1},{1,2},{2,3},{4,5},{5,6},{6,7},{8,9},{9,10},{10,11},{12,13},{... | collective-permute-start | bytes 12296 | tf_op jit(solution)/shard_map/ppermute | solution.py:26
  363.9 10.2 %collective-permute-start.31 = (f32[2,2,1,256]{3,2,1,0:T(1,128)S(1)}, f32[2,2,1,256]{3,2,1,0:T(1,128)S(1)}, u32[]{:S(2)}, u32[]{:S(2)}) collective-permute-start(f32[2,2,1,256]{3,2,1,0:T(1,128)S(1)} %get-tuple-element.6), channel_id=1, source_target_pairs={{1,0},{2,1},{3,2},{5,4},{6,5},{7,6},{9,8},{10,9},{11,10},{13,12},{... | collective-permute-start | bytes 12296 | tf_op jit(solution)/shard_map/ppermute | solution.py:28
  365.8 8.8 %collective-permute-start.32 = (f32[2,2,1,256]{3,2,1,0:T(1,128)S(1)}, f32[2,2,1,256]{3,2,1,0:T(1,128)S(1)}, u32[]{:S(2)}, u32[]{:S(2)}) collective-permute-start(f32[2,2,1,256]{3,2,1,0:T(1,128)S(1)} %get-tuple-element.5), channel_id=1, source_target_pairs={{0,1},{1,2},{2,3},{4,5},{5,6},{6,7},{8,9},{9,10},{10,11},{12,13},{... | collective-permute-start | bytes 12296 | tf_op jit(solution)/shard_map/ppermute | solution.py:26
Sparse Core Ops, SparseCore 0:
  181.2 81.6 all-reduce.1
where the time goes:
time: 384 us; the launch traced here: 382 us
  starting transfers between devices  181 us (47%)
  waiting for transfers between devices  104 us (27%)
  local copies, waits for them, and re-layouts  50.5 us (13%)
  blocking collectives  18.8 us (5%)
  between operations  14.4 us (4%)
  other arithmetic  12.1 us (3%)
    ppermute x16, starting transfers between devices, padded(): lax.ppermute(tail, axis, [(i, (i + 1) % count) for i in range(ends)])  123 us
    psum x1, waiting for transfers between devices, per_device(): increment = lax.psum(partial_sum, 'mem')  81.8 us
    ppermute x16, starting transfers between devices, padded(): lax.ppermute(head, axis, [((i + 1) % count, i) for i in range(ends)])  37.9 us
    unnamed x16, local copies, waits for them, and re-layouts  28.3 us
    all_to_all x1, blocking collectives, per_device(): lax.all_to_all(lifted_field, 'lev', split_axis=1, concat_axis=2, tiled=True)  18.8 us
    ppermute x1, starting transfers between devices, from_behind(): lax.ppermute(value, axis, [(source, source + steps) for source in range(i...  16.1 us
    all_to_all x3, local copies, waits for them, and re-layouts, per_device(): lax.all_to_all(smoothed_field, 'lev', split_axis=2, concat_axis=1, tiled=...  10.2 us
    all_to_all x1, waiting for transfers between devices, per_device(): lax.all_to_all(smoothed_field, 'lev', split_axis=2, concat_axis=1, tiled=...  9.28 us
  transfers between devices with their start and end apart: 35, of which 14 were waited for; matrix products, arithmetic and copies ran while one was open for 3% of the time, Pallas kernels for 0%

commit v1 on v0

v1 whole, which is shorter than its diff:
```python
import functools

import jax
import jax.numpy as jnp
from jax import lax
from jax.experimental import pallas as pl
from jax.experimental.pallas import tpu as pltpu
from jax.sharding import PartitionSpec as P

PASSES = 8
HUBER = 1.0
MESH = pl.DeviceIdType.MESH
F32 = jnp.float32

LANES = 128
SUB = 8
LATS = 32
HALO = 8
FIRST = HALO + 1
ROWS = LATS + 2 * FIRST
LEVS = 32
MEMS = 8
BLOCKS = 4
CHUNK = 16


def tiles(start, count):
    return pl.ds(pl.multiple_of(SUB * start, SUB), SUB * count)


def sublane(member, level, half):
    return 4 * half + 2 * member + level


def next_longitude(x, lane):
    turned = pltpu.roll(x, LANES - 1, 2)
    return jnp.where(lane == LANES - 1, pltpu.roll(turned, 4, 1), turned)


def previous_longitude(x, lane):
    turned = pltpu.roll(x, 1, 2)
    return jnp.where(lane == 0, pltpu.roll(turned, 4, 1), turned)


def diffuse(field, other, east, south, keep_lower):
    lane = lax.broadcasted_iota(jnp.int32, (8, SUB, LANES), 2)

    def rows_of(ref, start):
        return ref[tiles(start, 8), :].reshape(8, SUB, LANES)

    def one_pass(source, target):
        for chunk in range(LATS // 8 + 2):
            start = 1 + 8 * chunk
            center = rows_of(source, start)
            flux_x = rows_of(east, start) * (next_longitude(center, lane) - center)
            flux_in = rows_of(south, start) * (center - rows_of(source, start - 1))
            flux_out = rows_of(south, start + 1) * (rows_of(source, start + 1) - center)
            result = center + flux_x - previous_longitude(flux_x, lane) + flux_out - flux_in
            if chunk == 0:
                result = result * keep_lower
            target[tiles(start, 8), :] = result.reshape(8 * SUB, LANES)

    @pl.loop(0, PASSES // 2)
    def _(step):
        one_pass(field, other)
        one_pass(other, field)


def vertical_columns(band_ref, group_ref, out_ref):
    band = band_ref[...]
    group = group_ref[...]
    group = jnp.concatenate([group, group], axis=1)
    coefs = []
    for offset in range(-3, 4):
        coef = band[offset + 3 : offset + 4, :] + (1.0 if offset == 0 else 0.0)
        coef = jnp.concatenate([coef, coef], axis=1)
        ahead = group if offset == 0 else pltpu.roll(group, (-offset) % LANES, 1)
        coef = jnp.where(ahead == group, coef, 0.0)
        coefs.append(jnp.concatenate([coef, coef], axis=1))

    @pl.loop(0, 8)
    def _(part):
        shape = (32, 256)
        row = lax.broadcasted_iota(jnp.int32, shape, 0) + 32 * part
        col = lax.broadcasted_iota(jnp.int32, shape, 1)
        half, member, level = (row // 4) % 2, (row // 2) % 2, row % 2
        apart = 2 * (row // SUB) + level + 1024 * (2 * member + half) - col % 64 - 1024 * (col // 64)
        total = jnp.zeros(shape, F32)
        for offset in range(-3, 4):
            total = jnp.where(apart == offset, coefs[offset + 3], total)
        out_ref[pl.ds(pl.multiple_of(32 * part, 32), 32), :] = total


def kernel(
    control_hbm, members_hbm, east_hbm, south_hbm, innovation_hbm, huber_hbm, band_ref, group_ref,
    out_hbm,
    control, members, east_in, south_in, innovation, huber, out,
    east, south, field, other, lifted_field, east_edge, south_edge,
    gathered, lift, lower_matrix, upper_matrix,
    part_sums, parts, weighted, weighted_all,
    local_sems, edge_send, edge_recv, fwd_sems, sum_sems, share_sems, back_send, back_recv,
):
    m, l, r = lax.axis_index("mem"), lax.axis_index("lev"), lax.axis_index("row")
    has_lower = (r + BLOCKS - 1) // BLOCKS
    has_upper = 1 - (r + 1) // BLOCKS
    low_edge = 1 - (l + LEVS - HALO) // LEVS
    high_edge = (l + HALO) // LEVS

    def remote(source, target, send, recv, **where):
        return pltpu.make_async_remote_copy(
            src_ref=source, dst_ref=target, send_sem=send, recv_sem=recv,
            device_id=where, device_id_type=MESH,
        )

    barrier = pltpu.get_barrier_semaphore()

    def greet(**where):
        pl.semaphore_signal(barrier, inc=1, device_id=where, device_id_type=MESH)

    @pl.when(r > 0)
    def _():
        greet(row=r - 1)

    @pl.when(r < BLOCKS - 1)
    def _():
        greet(row=r + 1)

    @pl.loop(1, LEVS)
    def _(i):
        greet(lev=lax.rem(l + i, LEVS))

    @pl.loop(1, MEMS)
    def _(i):
        greet(mem=lax.rem(m + i, MEMS))

    @pl.when(r > 0)
    def _():
        @pl.loop(0, HALO)
        def _(i):
            greet(lev=LEVS - HALO + i, row=r - 1)

    @pl.when(r < BLOCKS - 1)
    def _():
        @pl.loop(0, HALO)
        def _(i):
            greet(lev=i, row=r + 1)

    mine = (
        pl.ds(pl.multiple_of(CHUNK * lax.rem(m, 4), CHUNK), CHUNK),
        pl.ds(pl.multiple_of(LANES * (m // 4), LANES), LANES),
    )
    loads = [
        pltpu.make_async_copy(source, target, local_sems.at[i])
        for i, (source, target) in enumerate([
            (control_hbm, control), (east_hbm, east_in), (south_hbm, south_in),
            (members_hbm, members),
            (innovation_hbm.at[mine[0], mine[1]], innovation),
            (huber_hbm.at[mine[0], mine[1]], huber),
        ])
    ]
    for load in loads:
        load.start()

    blank = jnp.zeros((HALO * SUB, LANES), F32)
    for ref in (east, south, field, other, lifted_field):
        ref[tiles(0, 1), :] = blank[:SUB]
        ref[tiles(ROWS - 1, 1), :] = blank[:SUB]

    @pl.when(r == 0)
    def _():
        for ref in (east, south, field, lifted_field):
            ref[tiles(1, HALO), :] = blank

    @pl.when(r == BLOCKS - 1)
    def _():
        for ref in (east, south, field, lifted_field):
            ref[tiles(FIRST + LATS, HALO), :] = blank

    loads[0].wait()
    for member in range(2):
        for level in range(2):
            own = control[member, level].astype(F32)
            for half in range(2):
                field[pl.ds(SUB * FIRST + sublane(member, level, half), LATS, stride=SUB), :] = own[
                    :, half * LANES : (half + 1) * LANES
                ]
    loads[1].wait()
    loads[2].wait()

    pl.semaphore_wait(
        barrier,
        LEVS - 1 + MEMS - 1 + has_lower + has_upper
        + LEVS * (low_edge * has_lower + high_edge * has_upper),
    )

    def edge_copies(side, row):
        edge = slice(0, HALO) if side == 0 else slice(LATS - HALO, LATS)
        first = FIRST if side == 0 else FIRST + LATS - HALO
        landing = FIRST + LATS if side == 0 else 1
        return [
            remote(field.at[tiles(first, HALO), :], field.at[tiles(landing, HALO), :],
                   edge_send.at[side, 0], edge_recv.at[side, 0], row=row),
            remote(east_in.at[:, edge, :], east_edge.at[side],
                   edge_send.at[side, 1], edge_recv.at[side, 1], row=row),
            remote(south_in.at[:, edge, :], south_edge.at[side],
                   edge_send.at[side, 2], edge_recv.at[side, 2], row=row),
        ]

    @pl.when(r > 0)
    def _():
        for copy in edge_copies(0, r - 1):
            copy.start()

    @pl.when(r < BLOCKS - 1)
    def _():
        for copy in edge_copies(1, r + 1):
            copy.start()

    def place(target, value, level, first, count):
        for half in range(2):
            for member in range(2):
                target[pl.ds(SUB * first + sublane(member, level, half), count, stride=SUB), :] = value[
                    :, half * LANES : (half + 1) * LANES
                ]

    for level in range(2):
        place(east, east_in[level], level, FIRST, LATS)
        place(south, south_in[level], level, FIRST, LATS)
    vertical_columns(band_ref, group_ref, upper_matrix)
    lower_matrix[...] = upper_matrix[...].T
    for load in loads[3:]:
        load.wait()

    def take_edge(side, first):
        for copy in edge_copies(side, r):
            copy.wait_recv()
        for level in range(2):
            place(east, east_edge[side, level], level, first, HALO)
            place(south, south_edge[side, level], level, first, HALO)

    @pl.when(r < BLOCKS - 1)
    def _():
        take_edge(0, FIRST + LATS)

    @pl.when(r > 0)
    def _():
        take_edge(1, 1)

    @pl.when(r > 0)
    def _():
        for copy in edge_copies(0, r - 1):
            copy.wait_send()

    @pl.when(r < BLOCKS - 1)
    def _():
        for copy in edge_copies(1, r + 1):
            copy.wait_send()

    keep_lower = has_lower.astype(F32)
    diffuse(field, other, east, south, keep_lower)

    @pl.loop(1, LEVS)
    def _(i):
        peer = lax.rem(l + i, LEVS)
        remote(field.at[tiles(FIRST + peer, 1), :], gathered.at[tiles(l, 1), :],
               fwd_sems.at[0], fwd_sems.at[1], lev=peer).start()

    gathered[tiles(l, 1), :] = field[tiles(FIRST + l, 1), :]
    everyone = remote(field.at[tiles(FIRST, LEVS - 1), :], gathered.at[tiles(0, LEVS - 1), :],
                      fwd_sems.at[0], fwd_sems.at[1], lev=l)
    everyone.wait_recv()

    filtered = jnp.dot(lower_matrix[...], gathered[...], precision=lax.Precision.HIGHEST,
                       preferred_element_type=F32)

    def member_columns(member, half):
        return members[member, :, half * LANES : (half + 1) * LANES].astype(F32)

    for half in range(2):
        term = sum(
            member_columns(member, half) * filtered[64 * (2 * member + half) : 64 * (2 * member + half + 1)]
            for member in range(2)
        )
        for quarter in range(4):
            part_sums[4 * half + quarter] = term[CHUNK * quarter : CHUNK * (quarter + 1)]

    @pl.loop(1, MEMS)
    def _(i):
        peer = lax.rem(m + i, MEMS)
        remote(part_sums.at[peer], parts.at[m], sum_sems.at[0], sum_sems.at[1], mem=peer).start()

    parts[m] = part_sums[m]
    all_parts = remote(part_sums.at[pl.ds(0, MEMS - 1)], parts.at[pl.ds(0, MEMS - 1)],
                       sum_sems.at[0], sum_sems.at[1], mem=m)
    all_parts.wait_recv()
    increment = parts[0]
    for i in range(1, MEMS):
        increment = increment + parts[i]
    residual = increment - innovation[...]
    scale = HUBER / jnp.maximum(jnp.abs(residual), HUBER)
    weighted[...] = jnp.where(huber[...] == 1, scale, 1.0) * residual

    @pl.loop(1, MEMS)
    def _(i):
        peer = lax.rem(m + i, MEMS)
        remote(weighted, weighted_all.at[m], share_sems.at[0], share_sems.at[1], mem=peer).start()

    weighted_all[m] = weighted[...]
    all_shares = remote(weighted_all.at[pl.ds(0, MEMS - 1)], weighted_all.at[pl.ds(0, MEMS - 1)],
                        share_sems.at[0], share_sems.at[1], mem=m)
    all_shares.wait_recv()

    columns = weighted_all[...].reshape(2, 64, LANES)
    adjoint = jnp.concatenate(
        [member_columns(member, half) * columns[half] for member in range(2) for half in range(2)], axis=0
    )
    lift[...] = jnp.dot(upper_matrix[...], adjoint, precision=lax.Precision.HIGHEST,
                        preferred_element_type=F32)

    def back(peer, landing, way, **where):
        return remote(lift.at[tiles(peer, 1), :], lifted_field.at[tiles(landing, 1), :],
                      back_send.at[way], back_recv.at[way], lev=peer, **where)

    @pl.when(low_edge * has_lower == 1)
    def _():
        @pl.loop(0, LEVS)
        def _(i):
            back(lax.rem(l + i, LEVS), FIRST + LATS + l, 1, row=r - 1).start()

    @pl.when(high_edge * has_upper == 1)
    def _():
        @pl.loop(0, LEVS)
        def _(i):
            back(lax.rem(l + i, LEVS), 1 + l - (LEVS - HALO), 2, row=r + 1).start()

    @pl.loop(1, LEVS)
    def _(i):
        back(lax.rem(l + i, LEVS), FIRST + l, 0).start()

    lifted_field[tiles(FIRST + l, 1), :] = lift[tiles(l, 1), :]

    def batch(way, count):
        return remote(lift.at[tiles(0, count), :], lift.at[tiles(0, count), :],
                      back_send.at[way], back_recv.at[way], lev=l)

    batch(0, LEVS - 1).wait_recv()

    @pl.when(r < BLOCKS - 1)
    def _():
        batch(1, HALO).wait_recv()

    @pl.when(r > 0)
    def _():
        batch(2, HALO).wait_recv()

    diffuse(lifted_field, other, east, south, keep_lower)

    for member in range(2):
        for level in range(2):
            for half in range(2):
                lanes = slice(half * LANES, (half + 1) * LANES)
                smooth = lifted_field[
                    pl.ds(SUB * FIRST + sublane(member, level, half), LATS, stride=SUB), :
                ]
                out[member, level, :, lanes] = control[member, level, :, lanes].astype(F32) + smooth

    store = pltpu.make_async_copy(out, out_hbm, local_sems.at[0])
    store.start()
    everyone.wait_send()
    all_parts.wait_send()
    all_shares.wait_send()
    batch(0, LEVS - 1).wait_send()

    @pl.when(low_edge * has_lower == 1)
    def _():
        batch(1, LEVS).wait_send()

    @pl.when(high_edge * has_upper == 1)
    def _():
        batch(2, LEVS).wait_send()

    store.wait()


def per_device(
    control, members, east_coef, south_coef, innovation, huber_class, band, level_group_index
):
    hbm = pl.BlockSpec(memory_space=pl.ANY)
    vmem = pl.BlockSpec(memory_space=pltpu.VMEM)
    dma = pltpu.SemaphoreType.DMA
    return pl.pallas_call(
        kernel,
        out_shape=jax.ShapeDtypeStruct(control.shape, F32),
        in_specs=[hbm] * 6 + [vmem] * 2,
        out_specs=hbm,
        scratch_shapes=[
            pltpu.VMEM(control.shape, jnp.bfloat16),
            pltpu.VMEM(members.shape, jnp.bfloat16),
            pltpu.VMEM(east_coef.shape, F32),
            pltpu.VMEM(south_coef.shape, F32),
            pltpu.VMEM((CHUNK, LANES), F32),
            pltpu.VMEM((CHUNK, LANES), jnp.int32),
            pltpu.VMEM(control.shape, F32),
            pltpu.VMEM((SUB * ROWS, LANES), F32),
            pltpu.VMEM((SUB * ROWS, LANES), F32),
            pltpu.VMEM((SUB * ROWS, LANES), F32),
            pltpu.VMEM((SUB * ROWS, LANES), F32),
            pltpu.VMEM((SUB * ROWS, LANES), F32),
            pltpu.VMEM((2, 2, HALO, 2 * LANES), F32),
            pltpu.VMEM((2, 2, HALO, 2 * LANES), F32),
            pltpu.VMEM((SUB * LEVS, LANES), F32),
            pltpu.VMEM((SUB * LEVS, LANES), F32),
            pltpu.VMEM((256, 256), F32),
            pltpu.VMEM((256, 256), F32),
            pltpu.VMEM((MEMS, CHUNK, LANES), F32),
            pltpu.VMEM((MEMS, CHUNK, LANES), F32),
            pltpu.VMEM((CHUNK, LANES), F32),
            pltpu.VMEM((MEMS, CHUNK, LANES), F32),
            dma((6,)),
            dma((2, 3)),
            dma((2, 3)),
            dma((2,)),
            dma((2,)),
            dma((2,)),
            dma((3,)),
            dma((3,)),
        ],
        compiler_params=pltpu.CompilerParams(collective_id=0, has_side_effects=True),
        name="hybrid_gradient",
    )(
        control, members, east_coef, south_coef, innovation, huber_class, band,
        level_group_index.reshape(1, -1),
    )


def solution(mesh):
    placed = (
        P("mem", "lev", "row", None),
        P("mem", None, ("row", "lev")),
        P("lev", "row", None),
        P("lev", "row", None),
        P(None, ("row", "lev")),
        P(None, ("row", "lev")),
        P(),
        P(),
    )
    return jax.shard_map(
        per_device,
        mesh=mesh,
        in_specs=placed,
        out_specs=P("mem", "lev", "row", None),
        check_vma=False,
    )
```

time: 384 us -> 62.5 us (0.16)
  starting transfers between devices: 181 us -> 0 us
  waiting for transfers between devices: 104 us -> 0 us
  Pallas kernels: 0 us -> 60.6 us
  local copies, waits for them, and re-layouts: 50.5 us -> 1.57 us
  blocking collectives: 18.8 us -> 0 us
  between operations: 14.4 us -> 0.01 us
  other arithmetic: 12.1 us -> 0 us
    ppermute x33 -> x0, starting transfers between devices: 177 us -> none  [the longest x16 123 us: padded(): lax.ppermute(tail, axis, [(i, (i + 1) % count) for i in range(ends)])]
    psum x1 -> x0, waiting for transfers between devices: 81.8 us -> none  [per_device(): increment = lax.psum(partial_sum, 'mem')]
    pallas_call x0 -> x1, Pallas kernels: none -> 60.6 us  [per_device(): pl.pallas_call(kernel, out_shape=jax.ShapeDtypeStruct(control.shape, F32)...]
    unnamed x16 -> x1, local copies, waits for them, and re-layouts: 28.3 us -> 1.57 us
    all_to_all x1 -> x0, blocking collectives: 18.8 us -> none  [per_device(): lax.all_to_all(lifted_field, 'lev', split_axis=1, concat_axis=2, tiled=True)]
    ppermute x33 -> x0, waiting for transfers between devices: 12.8 us -> none  [the longest x16 6.76 us: padded(): lax.ppermute(head, axis, [((i + 1) % count, i) for i in range(ends)])]
    all_to_all x4 -> x0, local copies, waits for them, and re-layouts: 10.2 us -> none  [the longest x3 10.2 us: per_device(): lax.all_to_all(smoothed_field, 'lev', split_axis=2, concat_axis=1, tiled=...]
    all_to_all x1 -> x0, waiting for transfers between devices: 9.28 us -> none  [per_device(): lax.all_to_all(smoothed_field, 'lev', split_axis=2, concat_axis=1, tiled=...]
  transfers between devices with their start and end apart: 35 -> 0, of which waited for: 14 -> 0; matrix products, arithmetic and copies ran while one was open for 3% -> 0% of each run, Pallas kernels for 0% -> 0%
where the time goes in v1:
time: 62.5 us; the launch traced here: 62.2 us
  Pallas kernels  60.6 us (97%)
  local copies, waits for them, and re-layouts  1.57 us (3%)
    pallas_call x1, Pallas kernels, per_device(): pl.pallas_call(kernel, out_shape=jax.ShapeDtypeStruct(control.shape, F32)...  60.6 us
    unnamed x1, local copies, waits for them, and re-layouts  1.57 us

profile of v1, /device:TPU:1, one launch (start us, length us, event | category | flops | bytes accessed | tf_op | source)
XLA Modules:
  0.0 62.2 jit_solution(12806931617871584502)
XLA Ops:
  0.0 60.6 %hybrid_gradient.1 = f32[2,2,32,256]{3,2,1,0:T(8,128)} custom-call(bf16[2,2,32,256]{3,2,1,0:T(8,128)(2,1)} %control_hbm.1, bf16[2,64,256]{2,1,0:T(8,128)(2,1)} %members_hbm.1, f32[2,32,256]{2,1,0:T(8,128)} %east_hbm.1, f32[2,32,256]{2,1,0:T(8,128)} %south_hbm.1, f32[64,256]{1,0:T(8,128)} %innovation_hbm.1, s32[64,256]{1,0:T(8,128)} %huber_hbm.1, ...), custom_call_target="tpu_custom_call" | custom-call | tf_op jit(solution)/shard_map/hybrid_gradient/pallas_call | solution.py:391
  60.7 1.6 %copy.10 = f32[2,2,32,256]{3,2,1,0:T(8,128)} copy(f32[2,2,32,256]{3,2,1,0:T(8,128)} %hybrid_gradient.1) | data formatting | bytes 262144

commit v2 on v1

v2 whole, which is shorter than its diff:
```python
import jax
import jax.numpy as jnp
from jax import lax
from jax.experimental import pallas as pl
from jax.experimental.pallas import tpu as pltpu
from jax.sharding import PartitionSpec as P

PASSES = 8
HUBER = 1.0
MESH = pl.DeviceIdType.MESH
F32 = jnp.float32

LANES = 128
SUB = 8
LATS = 32
HALO = 8
FIRST = HALO
ROWS = LATS + 2 * HALO
LEVS = 32
WIDE = 8
MEMS = 8
ROOT = MEMS - 1
BLOCKS = 4
FAR_FIRST = (4, 3, 5, 2, 6, 1, 7, 0)


def tiles(start, count):
    if isinstance(start, int):
        return pl.ds(SUB * start, SUB * count)
    return pl.ds(pl.multiple_of(SUB * start, SUB), SUB * count)


def sublane(member, level, half):
    return 4 * half + 2 * member + level


def next_longitude(x, lane):
    turned = pltpu.roll(x, LANES - 1, 2)
    return jnp.where(lane == LANES - 1, pltpu.roll(turned, 4, 1), turned)


def previous_longitude(x, lane):
    turned = pltpu.roll(x, 1, 2)
    return jnp.where(lane == 0, pltpu.roll(turned, 4, 1), turned)


def lane_index():
    return lax.broadcasted_iota(jnp.int32, (8, SUB, LANES), 2)


def one_pass(fields, coefs, step, start):
    east, west, south = coefs
    lane = lane_index()

    def field(row):
        return fields[step - 1, tiles(row, 8), :].reshape(8, SUB, LANES)

    def coef(ref, row):
        return ref[tiles(row, 8), :].reshape(8, SUB, LANES)

    center = field(start)
    flux_x = coef(east, start) * (next_longitude(center, lane) - center)
    flux_west = coef(west, start) * (center - previous_longitude(center, lane))
    flux_in = coef(south, start) * (center - field(start - 1))
    flux_out = coef(south, start + 1) * (field(start + 1) - center)
    return center + flux_x - flux_west + flux_out - flux_in


def diffuse_inside(fields, coefs):
    for step in range(1, PASSES + 1):
        starts = list(range(step, 24 - step, 8)) + [24 - step]
        for start in starts:
            result = one_pass(fields, coefs, step, FIRST + start)
            fields[step, tiles(FIRST + start, 8), :] = result.reshape(8 * SUB, LANES)


def diffuse_edges(fields, coefs, keep_lower):
    row = lax.broadcasted_iota(jnp.int32, (8, SUB, LANES), 0)

    @pl.loop(1, PASSES + 1)
    def _(step):
        low, high = FIRST - HALO + step, FIRST + LATS - step
        lower = one_pass(fields, coefs, step, low)
        upper = one_pass(fields, coefs, step, high)
        lower = lower * jnp.where(row + low >= FIRST, 1.0, keep_lower)
        fields[step, tiles(low, 8), :] = lower.reshape(8 * SUB, LANES)
        fields[step, tiles(high, 8), :] = upper.reshape(8 * SUB, LANES)


def vertical_columns(band_ref, group_ref, out_ref):
    band = band_ref[...]
    group = group_ref[...]
    group = jnp.concatenate([group, group], axis=1)
    coefs = []
    for offset in range(-3, 4):
        coef = band[offset + 3 : offset + 4, :] + (1.0 if offset == 0 else 0.0)
        coef = jnp.concatenate([coef, coef], axis=1)
        ahead = group if offset == 0 else pltpu.roll(group, (-offset) % LANES, 1)
        coef = jnp.where(ahead == group, coef, 0.0)
        coefs.append(jnp.concatenate([coef, coef], axis=1))

    @pl.loop(0, 8)
    def _(part):
        shape = (32, 256)
        row = lax.broadcasted_iota(jnp.int32, shape, 0) + 32 * part
        col = lax.broadcasted_iota(jnp.int32, shape, 1)
        half, member, level = (row // 4) % 2, (row // 2) % 2, row % 2
        apart = 2 * (row // SUB) + level + 1024 * (2 * member + half) - col % 64 - 1024 * (col // 64)
        total = jnp.zeros(shape, F32)
        for offset in range(-3, 4):
            total = jnp.where(apart == offset, coefs[offset + 3], total)
        out_ref[pl.ds(pl.multiple_of(32 * part, 32), 32), :] = total


def kernel(
    control_hbm, members_hbm, east_hbm, south_hbm, innovation_hbm, huber_hbm, band_hbm, group_hbm,
    out_hbm,
    control, members, east_in, south_in, innovation, huber, band, group, out,
    east, west, south, fields, back_fields, east_edge, south_edge,
    gathered, lift, relay, lower_matrix, upper_matrix,
    term, parts, share,
    local_sems, edge_send, edge_recv, fwd_sems, sum_sems, share_sems,
    back_sems, block_sems, relay_sems, lev_ready, mem_ready,
):
    m, l, r = lax.axis_index("mem"), lax.axis_index("lev"), lax.axis_index("row")
    along, across = l // WIDE, lax.rem(l, WIDE)
    has_lower = (r + BLOCKS - 1) // BLOCKS
    has_upper = 1 - (r + 1) // BLOCKS
    low_edge = 1 - (l + LEVS - HALO) // LEVS
    high_edge = (l + HALO) // LEVS
    from_low = low_edge * has_lower
    from_high = high_edge * has_upper
    coefs = (east, west, south)

    def leader(row):
        return 28 - 24 * (row // 2)

    is_leader = jnp.where(l == leader(r), 1, 0)
    is_root = m // ROOT

    def remote(source, target, send, recv, **where):
        return pltpu.make_async_remote_copy(
            src_ref=source, dst_ref=target, send_sem=send, recv_sem=recv,
            device_id=where, device_id_type=MESH,
        )

    barrier = pltpu.get_barrier_semaphore()

    def tell(sem, **where):
        pl.semaphore_signal(sem, inc=1, device_id=where, device_id_type=MESH)

    @pl.when(r > 0)
    def _():
        tell(barrier, row=r - 1)

    @pl.when(r < BLOCKS - 1)
    def _():
        tell(barrier, row=r + 1)

    @pl.when(is_leader == 0)
    def _():
        tell(barrier, lev=leader(r))

    @pl.when(is_root == 0)
    def _():
        tell(barrier, mem=ROOT)

    @pl.when(from_low == 1)
    def _():
        tell(barrier, lev=leader(r - 1), row=r - 1)

    @pl.when(from_high == 1)
    def _():
        tell(barrier, lev=leader(r + 1), row=r + 1)

    loads = [
        pltpu.make_async_copy(source, target, local_sems.at[i])
        for i, (source, target) in enumerate([
            (control_hbm, control), (east_hbm, east_in), (south_hbm, south_in),
            (band_hbm, band), (group_hbm, group),
            (members_hbm, members), (innovation_hbm, innovation), (huber_hbm, huber),
        ])
    ]
    for load in loads:
        load.start()

    blank = jnp.zeros((HALO * SUB, LANES), F32)
    halo_refs = (east, west, south, fields.at[0], back_fields.at[0])

    @pl.when(r == 0)
    def _():
        for ref in halo_refs:
            ref[tiles(0, HALO), :] = blank

    @pl.when(r == BLOCKS - 1)
    def _():
        for ref in halo_refs:
            ref[tiles(FIRST + LATS, HALO), :] = blank

    loads[0].wait()
    for member in range(2):
        for level in range(2):
            own = control[member, level].astype(F32)
            for half in range(2):
                fields[0, pl.ds(SUB * FIRST + sublane(member, level, half), LATS, stride=SUB), :] = own[
                    :, half * LANES : (half + 1) * LANES
                ]
    loads[1].wait()
    loads[2].wait()

    pl.semaphore_wait(
        barrier,
        has_lower + has_upper + is_root * (MEMS - 1)
        + is_leader * (LEVS - 1 + HALO * (has_lower + has_upper)),
    )

    def edge_copies(side, row):
        edge = slice(0, HALO) if side == 0 else slice(LATS - HALO, LATS)
        first = FIRST if side == 0 else FIRST + LATS - HALO
        landing = FIRST + LATS if side == 0 else 0
        return [
            remote(fields.at[0, tiles(first, HALO), :], fields.at[0, tiles(landing, HALO), :],
                   edge_send.at[side, 0], edge_recv.at[side, 0], row=row),
            remote(east_in.at[:, edge, :], east_edge.at[side],
                   edge_send.at[side, 1], edge_recv.at[side, 1], row=row),
            remote(south_in.at[:, edge, :], south_edge.at[side],
                   edge_send.at[side, 2], edge_recv.at[side, 2], row=row),
        ]

    @pl.when(r > 0)
    def _():
        for copy in edge_copies(0, r - 1):
            copy.start()

    @pl.when(r < BLOCKS - 1)
    def _():
        for copy in edge_copies(1, r + 1):
            copy.start()

    @pl.when(is_leader == 1)
    def _():
        @pl.loop(1, LEVS)
        def _(i):
            tell(lev_ready, lev=lax.rem(l + i, LEVS))

        @pl.when(r < BLOCKS - 1)
        def _():
            @pl.loop(0, HALO)
            def _(i):
                tell(lev_ready, lev=i, row=r + 1)

        @pl.when(r > 0)
        def _():
            @pl.loop(0, HALO)
            def _(i):
                tell(lev_ready, lev=LEVS - HALO + i, row=r - 1)

    @pl.when(is_root == 1)
    def _():
        @pl.loop(0, MEMS - 1)
        def _(i):
            tell(mem_ready, mem=i)

    def place(target, value, level, first, count):
        for half in range(2):
            for member in range(2):
                target[pl.ds(SUB * first + sublane(member, level, half), count, stride=SUB), :] = value[
                    :, half * LANES : (half + 1) * LANES
                ]

    def set_west(first):
        value = east[tiles(first, 8), :].reshape(8, SUB, LANES)
        west[tiles(first, 8), :] = previous_longitude(value, lane_index()).reshape(8 * SUB, LANES)

    for level in range(2):
        place(east, east_in[level], level, FIRST, LATS)
        place(south, south_in[level], level, FIRST, LATS)
    for first in range(FIRST, FIRST + LATS, 8):
        set_west(first)
    diffuse_inside(fields, coefs)

    pl.semaphore_wait(lev_ready, 1 - is_leader + from_low + from_high)

    def send_latitudes(rows):
        for apart in FAR_FIRST:
            for row in rows:
                peer = WIDE * row + lax.rem(across + apart, WIDE)

                def send(peer=peer):
                    remote(fields.at[PASSES, tiles(FIRST + peer, 1), :], gathered.at[tiles(l, 1), :],
                           fwd_sems.at[0], fwd_sems.at[1], lev=peer).start()

                if apart:
                    send()
                else:
                    pl.when(along != row)(send)

    send_latitudes((1, 2))

    for load in loads[3:]:
        load.wait()
    vertical_columns(band, group, upper_matrix)
    lower_matrix[...] = upper_matrix[...].T

    def take_edge(side, first):
        for copy in edge_copies(side, r):
            copy.wait_recv()
        for level in range(2):
            place(east, east_edge[side, level], level, first, HALO)
            place(south, south_edge[side, level], level, first, HALO)
        set_west(first)

    @pl.when(r < BLOCKS - 1)
    def _():
        take_edge(0, FIRST + LATS)

    @pl.when(r > 0)
    def _():
        take_edge(1, 0)

    keep_lower = has_lower.astype(F32)
    diffuse_edges(fields, coefs, keep_lower)
    send_latitudes((0, 3))

    gathered[tiles(l, 1), :] = fields[PASSES, tiles(FIRST + l, 1), :]
    everyone = remote(fields.at[PASSES, tiles(FIRST, LEVS - 1), :], gathered.at[tiles(0, LEVS - 1), :],
                      fwd_sems.at[0], fwd_sems.at[1], lev=l)
    everyone.wait_recv()

    filtered = jnp.dot(lower_matrix[...], gathered[...], precision=lax.Precision.HIGHEST,
                       preferred_element_type=F32)

    def member_columns(member, half):
        return members[member, :, half * LANES : (half + 1) * LANES].astype(F32)

    for half in range(2):
        term[half] = sum(
            member_columns(member, half) * filtered[64 * (2 * member + half) : 64 * (2 * member + half + 1)]
            for member in range(2)
        )

    def term_copy(half):
        return remote(term.at[half], parts.at[m, half], sum_sems.at[0, half], sum_sems.at[1, half], mem=ROOT)

    def share_copy(half, mem):
        return remote(share.at[half], share.at[half], share_sems.at[0, half], share_sems.at[1, half], mem=mem)

    def term_batch(half):
        return remote(parts.at[pl.ds(0, MEMS - 1), half], parts.at[pl.ds(0, MEMS - 1), half],
                      sum_sems.at[0, half], sum_sems.at[1, half], mem=ROOT)

    @pl.when(is_root == 0)
    def _():
        pl.semaphore_wait(mem_ready, 1)
        for half in range(2):
            term_copy(half).start()
        for half in range(2):
            share_copy(half, ROOT).wait_recv()

    @pl.when(is_root == 1)
    def _():
        for half in range(2):
            term_batch(half).wait_recv()
            increment = parts[0, half]
            for i in range(1, MEMS - 1):
                increment = increment + parts[i, half]
            increment = increment + term[half]
            lanes = slice(half * LANES, (half + 1) * LANES)
            residual = increment - innovation[:, lanes]
            scale = HUBER / jnp.maximum(jnp.abs(residual), HUBER)
            share[half] = jnp.where(huber[:, lanes] == 1, scale, 1.0) * residual
            for mem in (0, 6):
                share_copy(half, mem).start()
        for mem in (1, 5, 2, 4, 3):
            for half in range(2):
                share_copy(half, mem).start()

    adjoint = jnp.concatenate(
        [member_columns(member, half) * share[half] for member in range(2) for half in range(2)], axis=0
    )
    lift[...] = jnp.dot(upper_matrix[...], adjoint, precision=lax.Precision.HIGHEST,
                        preferred_element_type=F32)

    def block_copy(side, position, row):
        return remote(lift.at[tiles(WIDE * position, WIDE), :], relay.at[side],
                      block_sems.at[side, 0], block_sems.at[side, 1],
                      lev=WIDE * position + across, row=row)

    @pl.when(from_low == 1)
    def _():
        for position in (3, 2, 1, 0):
            block_copy(0, position, r - 1).start()

    @pl.when(from_high == 1)
    def _():
        for position in range(4):
            block_copy(1, position, r + 1).start()

    for apart in FAR_FIRST:
        for turn in range(4):
            if apart or turn:
                peer = WIDE * lax.rem(along + turn, 4) + lax.rem(across + apart, WIDE)
                remote(lift.at[tiles(peer, 1), :], back_fields.at[0, tiles(FIRST + l, 1), :],
                       back_sems.at[0], back_sems.at[1], lev=peer).start()

    back_fields[0, tiles(FIRST + l, 1), :] = lift[tiles(l, 1), :]

    def landing(side):
        return FIRST + LATS if side == 0 else 0

    def hand_on(side):
        block_copy(side, along, r).wait_recv()
        for apart in FAR_FIRST[:-1]:
            column = lax.rem(across + apart, WIDE)
            remote(relay.at[side, tiles(column, 1), :],
                   back_fields.at[0, tiles(landing(side) + across, 1), :],
                   relay_sems.at[side, 0], relay_sems.at[side, 1], lev=WIDE * along + column).start()
        back_fields[0, tiles(landing(side) + across, 1), :] = relay[side, tiles(across, 1), :]

    def handed(side):
        return remote(relay.at[side, tiles(0, WIDE - 1), :],
                      back_fields.at[0, tiles(landing(side), WIDE - 1), :],
                      relay_sems.at[side, 0], relay_sems.at[side, 1], lev=l)

    @pl.when(r > 0)
    def _():
        hand_on(1)

    @pl.when(r < BLOCKS - 1)
    def _():
        hand_on(0)

    columns = remote(lift.at[tiles(0, LEVS - 1), :], back_fields.at[0, tiles(FIRST, LEVS - 1), :],
                     back_sems.at[0], back_sems.at[1], lev=l)
    columns.wait_recv()
    diffuse_inside(back_fields, coefs)

    @pl.when(r > 0)
    def _():
        handed(1).wait_recv()

    @pl.when(r < BLOCKS - 1)
    def _():
        handed(0).wait_recv()

    diffuse_edges(back_fields, coefs, keep_lower)

    for member in range(2):
        for level in range(2):
            for half in range(2):
                lanes = slice(half * LANES, (half + 1) * LANES)
                smooth = back_fields[
                    PASSES, pl.ds(SUB * FIRST + sublane(member, level, half), LATS, stride=SUB), :
                ]
                out[member, level, :, lanes] = control[member, level, :, lanes].astype(F32) + smooth

    store = pltpu.make_async_copy(out, out_hbm, local_sems.at[0])
    store.start()

    @pl.when(r > 0)
    def _():
        for copy in edge_copies(0, r - 1):
            copy.wait_send()
        handed(1).wait_send()

    @pl.when(r < BLOCKS - 1)
    def _():
        for copy in edge_copies(1, r + 1):
            copy.wait_send()
        handed(0).wait_send()

    everyone.wait_send()

    @pl.when(is_root == 0)
    def _():
        for half in range(2):
            term_copy(half).wait_send()

    @pl.when(is_root == 1)
    def _():
        for half in range(2):
            term_batch_like = remote(parts.at[pl.ds(0, MEMS - 1), half], parts.at[pl.ds(0, MEMS - 1), half],
                                     share_sems.at[0, half], share_sems.at[1, half], mem=ROOT)
            term_batch_like.wait_send()

    def blocks_sent(side):
        return remote(lift.at[tiles(0, LEVS), :], lift.at[tiles(0, LEVS), :],
                      block_sems.at[side, 0], block_sems.at[side, 1], lev=l)

    @pl.when(from_low == 1)
    def _():
        blocks_sent(0).wait_send()

    @pl.when(from_high == 1)
    def _():
        blocks_sent(1).wait_send()

    columns.wait_send()
    store.wait()


def per_device(
    control, members, east_coef, south_coef, innovation, huber_class, band, level_group_index
):
    hbm = pl.BlockSpec(memory_space=pl.ANY)
    dma = pltpu.SemaphoreType.DMA
    group = level_group_index.reshape(1, -1)
    rows = pltpu.VMEM((SUB * ROWS, LANES), F32)
    return pl.pallas_call(
        kernel,
        out_shape=jax.ShapeDtypeStruct(control.shape, F32),
        in_specs=[hbm] * 8,
        out_specs=hbm,
        scratch_shapes=[
            pltpu.VMEM(control.shape, jnp.bfloat16),
            pltpu.VMEM(members.shape, jnp.bfloat16),
            pltpu.VMEM(east_coef.shape, F32),
            pltpu.VMEM(south_coef.shape, F32),
            pltpu.VMEM(innovation.shape, F32),
            pltpu.VMEM(huber_class.shape, jnp.int32),
            pltpu.VMEM(band.shape, F32),
            pltpu.VMEM(group.shape, jnp.int32),
            pltpu.VMEM(control.shape, F32),
            rows,
            rows,
            rows,
            pltpu.VMEM((PASSES + 1, SUB * ROWS, LANES), F32),
            pltpu.VMEM((PASSES + 1, SUB * ROWS, LANES), F32),
            pltpu.VMEM((2, 2, HALO, 2 * LANES), F32),
            pltpu.VMEM((2, 2, HALO, 2 * LANES), F32),
            pltpu.VMEM((SUB * LEVS, LANES), F32),
            pltpu.VMEM((SUB * LEVS, LANES), F32),
            pltpu.VMEM((2, SUB * WIDE, LANES), F32),
            pltpu.VMEM((256, 256), F32),
            pltpu.VMEM((256, 256), F32),
            pltpu.VMEM((2, 64, LANES), F32),
            pltpu.VMEM((MEMS - 1, 2, 64, LANES), F32),
            pltpu.VMEM((2, 64, LANES), F32),
            dma((8,)),
            dma((2, 3)),
            dma((2, 3)),
            dma((2,)),
            dma((2, 2)),
            dma((2, 2)),
            dma((2,)),
            dma((2, 2)),
            dma((2, 2)),
            pltpu.SemaphoreType.REGULAR,
            pltpu.SemaphoreType.REGULAR,
        ],
        compiler_params=pltpu.CompilerParams(collective_id=0, has_side_effects=True),
        name="hybrid_gradient",
    )(control, members, east_coef, south_coef, innovation, huber_class, band, group)


def solution(mesh):
    placed = (
        P("mem", "lev", "row", None),
        P("mem", None, ("row", "lev")),
        P("lev", "row", None),
        P("lev", "row", None),
        P(None, ("row", "lev")),
        P(None, ("row", "lev")),
        P(),
        P(),
    )
    return jax.shard_map(
        per_device,
        mesh=mesh,
        in_specs=placed,
        out_specs=P("mem", "lev", "row", None),
        check_vma=False,
    )
```

time: 62.5 us -> 55.4 us (0.89)
  Pallas kernels: 60.6 us -> 53.6 us
    pallas_call x1, Pallas kernels: 60.6 us -> 53.6 us  [per_device(): pl.pallas_call(kernel, out_shape=jax.ShapeDtypeStruct(control.shape, F32)...]
where the time goes in v2:
time: 55.4 us; the launch traced here: 55.2 us
  Pallas kernels  53.6 us (97%)
  local copies, waits for them, and re-layouts  1.57 us (3%)
    pallas_call x1, Pallas kernels, per_device(): pl.pallas_call(kernel, out_shape=jax.ShapeDtypeStruct(control.shape, F32)...  53.6 us
    unnamed x1, local copies, waits for them, and re-layouts  1.57 us

profile of v2, /device:TPU:1, one launch (start us, length us, event | category | flops | bytes accessed | tf_op | source)
XLA Modules:
  0.0 55.2 jit_solution(8705556112442988419)
XLA Ops:
  0.0 53.6 %hybrid_gradient.1 = f32[2,2,32,256]{3,2,1,0:T(8,128)} custom-call(bf16[2,2,32,256]{3,2,1,0:T(8,128)(2,1)} %control_hbm.1, bf16[2,64,256]{2,1,0:T(8,128)(2,1)} %members_hbm.1, f32[2,32,256]{2,1,0:T(8,128)} %east_hbm.1, f32[2,32,256]{2,1,0:T(8,128)} %south_hbm.1, f32[64,256]{1,0:T(8,128)} %innovation_hbm.1, s32[64,256]{1,0:T(8,128)} %huber_hbm.1, ...), custom_call_target="tpu_custom_call" | custom-call | tf_op jit(solution)/shard_map/hybrid_gradient/pallas_call | solution.py:509
  53.6 1.6 %copy.10 = f32[2,2,32,256]{3,2,1,0:T(8,128)} copy(f32[2,2,32,256]{3,2,1,0:T(8,128)} %hybrid_gradient.1) | data formatting | bytes 262144

commit v3 on v2

--- a/solution.py
+++ b/solution.py
@@ -112,12 +112,29 @@
         out_ref[pl.ds(pl.multiple_of(32 * part, 32), 32), :] = total
 
 
+def two_parts(x):
+    high = x.astype(jnp.bfloat16)
+    return high, (x - high.astype(F32)).astype(jnp.bfloat16)
+
+
+def split_matrix(matrix, out_ref):
+    high, low = two_parts(matrix)
+    out_ref[:, 0:256] = high
+    out_ref[:, 256:512] = high
+    out_ref[:, 512:768] = low
+
+
+def product(matrix_ref, x):
+    high, low = two_parts(x)
+    return jnp.dot(matrix_ref[...], jnp.concatenate([high, low, high], axis=0), preferred_element_type=F32)
+
+
 def kernel(
     control_hbm, members_hbm, east_hbm, south_hbm, innovation_hbm, huber_hbm, band_hbm, group_hbm,
     out_hbm,
     control, members, east_in, south_in, innovation, huber, band, group, out,
     east, west, south, fields, back_fields, east_edge, south_edge,
-    gathered, lift, relay, lower_matrix, upper_matrix,
+    gathered, lift, relay, full_matrix, lower_matrix, upper_matrix,
     term, parts, share,
     local_sems, edge_send, edge_recv, fwd_sems, sum_sems, share_sems,
     back_sems, block_sems, relay_sems, lev_ready, mem_ready,
@@ -299,8 +316,9 @@
 
     for load in loads[3:]:
         load.wait()
-    vertical_columns(band, group, upper_matrix)
-    lower_matrix[...] = upper_matrix[...].T
+    vertical_columns(band, group, full_matrix)
+    split_matrix(full_matrix[...], upper_matrix)
+    split_matrix(full_matrix[...].T, lower_matrix)
 
     def take_edge(side, first):
         for copy in edge_copies(side, r):
@@ -327,8 +345,7 @@
                       fwd_sems.at[0], fwd_sems.at[1], lev=l)
     everyone.wait_recv()
 
-    filtered = jnp.dot(lower_matrix[...], gathered[...], precision=lax.Precision.HIGHEST,
-                       preferred_element_type=F32)
+    filtered = product(lower_matrix, gathered[...])
 
     def member_columns(member, half):
         return members[member, :, half * LANES : (half + 1) * LANES].astype(F32)
@@ -339,62 +356,88 @@
             for member in range(2)
         )
 
+    roots = (ROOT, 0)
+    orders = ((0, 6, 1, 5, 2, 4, 3), (1, 7, 2, 6, 3, 5, 4))
+
     def term_copy(half):
-        return remote(term.at[half], parts.at[m, half], sum_sems.at[0, half], sum_sems.at[1, half], mem=ROOT)
+        return remote(term.at[half], parts.at[m - half, half], sum_sems.at[0, half], sum_sems.at[1, half],
+                      mem=roots[half])
 
     def share_copy(half, mem):
         return remote(share.at[half], share.at[half], share_sems.at[0, half], share_sems.at[1, half], mem=mem)
 
-    def term_batch(half):
-        return remote(parts.at[pl.ds(0, MEMS - 1), half], parts.at[pl.ds(0, MEMS - 1), half],
-                      sum_sems.at[0, half], sum_sems.at[1, half], mem=ROOT)
+    def rest(half, sems):
+        others = parts.at[pl.ds(0, MEMS - 1), half]
+        return remote(others, others, sems.at[0, half], sems.at[1, half], mem=m)
+
+    def gather_half(half):
+        rest(half, sum_sems).wait_recv()
+        values = [parts[i, half] for i in range(MEMS - 1)]
+        values.insert(roots[half], term[half])
+        increment = values[0]
+        for value in values[1:]:
+            increment = increment + value
+        lanes = slice(half * LANES, (half + 1) * LANES)
+        residual = increment - innovation[:, lanes]
+        scale = HUBER / jnp.maximum(jnp.abs(residual), HUBER)
+        share[half] = jnp.where(huber[:, lanes] == 1, scale, 1.0) * residual
+        for mem in orders[half]:
+            share_copy(half, mem).start()
 
     @pl.when(is_root == 0)
     def _():
         pl.semaphore_wait(mem_ready, 1)
+        term_copy(0).start()
+
+    @pl.when(m > 0)
+    def _():
+        term_copy(1).start()
+
+    @pl.when(is_root == 1)
+    def _():
+        gather_half(0)
+        share_copy(1, 0).wait_recv()
+
+    @pl.when(m == 0)
+    def _():
+        gather_half(1)
+        share_copy(0, 0).wait_recv()
+
+    @pl.when((m > 0) & (is_root == 0))
+    def _():
         for half in range(2):
-            term_copy(half).start()
-        for half in range(2):
-            share_copy(half, ROOT).wait_recv()
-
-    @pl.when(is_root == 1)
-    def _():
-        for half in range(2):
-            term_batch(half).wait_recv()
-            increment = parts[0, half]
-            for i in range(1, MEMS - 1):
-                increment = increment + parts[i, half]
-            increment = increment + term[half]
-            lanes = slice(half * LANES, (half + 1) * LANES)
-            residual = increment - innovation[:, lanes]
-            scale = HUBER / jnp.maximum(jnp.abs(residual), HUBER)
-            share[half] = jnp.where(huber[:, lanes] == 1, scale, 1.0) * residual
-            for mem in (0, 6):
-                share_copy(half, mem).start()
-        for mem in (1, 5, 2, 4, 3):
-            for half in range(2):
-                share_copy(half, mem).start()
+            share_copy(half, 0).wait_recv()
 
     adjoint = jnp.concatenate(
         [member_columns(member, half) * share[half] for member in range(2) for half in range(2)], axis=0
     )
-    lift[...] = jnp.dot(upper_matrix[...], adjoint, precision=lax.Precision.HIGHEST,
-                        preferred_element_type=F32)
+    lift[...] = product(upper_matrix, adjoint)
 
     def block_copy(side, position, row):
         return remote(lift.at[tiles(WIDE * position, WIDE), :], relay.at[side],
                       block_sems.at[side, 0], block_sems.at[side, 1],
                       lev=WIDE * position + across, row=row)
 
+    def landing(side):
+        return FIRST + LATS if side == 0 else 0
+
+    def direct_copy(side, column, row):
+        return remote(lift.at[tiles(column, 1), :], back_fields.at[0, tiles(landing(side) + across, 1), :],
+                      block_sems.at[side, 2], relay_sems.at[side, 1], lev=column, row=row)
+
+    def send_edges(side, positions, row):
+        for apart in FAR_FIRST:
+            direct_copy(side, lax.rem(across + apart, WIDE), row).start()
+        for position in positions:
+            block_copy(side, position, row).start()
+
     @pl.when(from_low == 1)
     def _():
-        for position in (3, 2, 1, 0):
-            block_copy(0, position, r - 1).start()
+        send_edges(0, (1, 2, 3), r - 1)
 
     @pl.when(from_high == 1)
     def _():
-        for position in range(4):
-            block_copy(1, position, r + 1).start()
+        send_edges(1, (3, 2, 1), r + 1)
 
     for apart in FAR_FIRST:
         for turn in range(4):
@@ -404,9 +447,6 @@
                        back_sems.at[0], back_sems.at[1], lev=peer).start()
 
     back_fields[0, tiles(FIRST + l, 1), :] = lift[tiles(l, 1), :]
-
-    def landing(side):
-        return FIRST + LATS if side == 0 else 0
 
     def hand_on(side):
         block_copy(side, along, r).wait_recv()
@@ -417,16 +457,16 @@
                    relay_sems.at[side, 0], relay_sems.at[side, 1], lev=WIDE * along + column).start()
         back_fields[0, tiles(landing(side) + across, 1), :] = relay[side, tiles(across, 1), :]
 
-    def handed(side):
-        return remote(relay.at[side, tiles(0, WIDE - 1), :],
-                      back_fields.at[0, tiles(landing(side), WIDE - 1), :],
+    def handed(side, count):
+        return remote(relay.at[side, tiles(0, count), :],
+                      back_fields.at[0, tiles(landing(side), count), :],
                       relay_sems.at[side, 0], relay_sems.at[side, 1], lev=l)
 
-    @pl.when(r > 0)
+    @pl.when((r > 0) & (along > 0))
     def _():
         hand_on(1)
 
-    @pl.when(r < BLOCKS - 1)
+    @pl.when((r < BLOCKS - 1) & (along > 0))
     def _():
         hand_on(0)
 
@@ -435,13 +475,22 @@
     columns.wait_recv()
     diffuse_inside(back_fields, coefs)
 
+    def halo_arrived(side):
+        @pl.when(along > 0)
+        def _():
+            handed(side, WIDE - 1).wait_recv()
+
+        @pl.when(along == 0)
+        def _():
+            handed(side, WIDE).wait_recv()
+
     @pl.when(r > 0)
     def _():
-        handed(1).wait_recv()
+        halo_arrived(1)
 
     @pl.when(r < BLOCKS - 1)
     def _():
-        handed(0).wait_recv()
+        halo_arrived(0)
 
     diffuse_edges(back_fields, coefs, keep_lower)
 
@@ -461,39 +510,50 @@
     def _():
         for copy in edge_copies(0, r - 1):
             copy.wait_send()
-        handed(1).wait_send()
+
+        @pl.when(along > 0)
+        def _():
+            handed(1, WIDE - 1).wait_send()
 
     @pl.when(r < BLOCKS - 1)
     def _():
         for copy in edge_copies(1, r + 1):
             copy.wait_send()
-        handed(0).wait_send()
+
+        @pl.when(along > 0)
+        def _():
+            handed(0, WIDE - 1).wait_send()
 
     everyone.wait_send()
 
     @pl.when(is_root == 0)
     def _():
-        for half in range(2):
-            term_copy(half).wait_send()
+        term_copy(0).wait_send()
+
+    @pl.when(m > 0)
+    def _():
+        term_copy(1).wait_send()
 
     @pl.when(is_root == 1)
     def _():
-        for half in range(2):
-            term_batch_like = remote(parts.at[pl.ds(0, MEMS - 1), half], parts.at[pl.ds(0, MEMS - 1), half],
-                                     share_sems.at[0, half], share_sems.at[1, half], mem=ROOT)
-            term_batch_like.wait_send()
-
-    def blocks_sent(side):
-        return remote(lift.at[tiles(0, LEVS), :], lift.at[tiles(0, LEVS), :],
-                      block_sems.at[side, 0], block_sems.at[side, 1], lev=l)
+        rest(0, share_sems).wait_send()
+
+    @pl.when(m == 0)
+    def _():
+        rest(1, share_sems).wait_send()
+
+    def edges_sent(side):
+        for way, count in ((0, LEVS - WIDE), (2, WIDE)):
+            remote(lift.at[tiles(0, count), :], lift.at[tiles(0, count), :],
+                   block_sems.at[side, way], block_sems.at[side, 1], lev=l).wait_send()
 
     @pl.when(from_low == 1)
     def _():
-        blocks_sent(0).wait_send()
+        edges_sent(0)
 
     @pl.when(from_high == 1)
     def _():
-        blocks_sent(1).wait_send()
+        edges_sent(1)
 
     columns.wait_send()
     store.wait()
@@ -532,7 +592,8 @@
             pltpu.VMEM((SUB * LEVS, LANES), F32),
             pltpu.VMEM((2, SUB * WIDE, LANES), F32),
             pltpu.VMEM((256, 256), F32),
-            pltpu.VMEM((256, 256), F32),
+            pltpu.VMEM((256, 768), jnp.bfloat16),
+            pltpu.VMEM((256, 768), jnp.bfloat16),
             pltpu.VMEM((2, 64, LANES), F32),
             pltpu.VMEM((MEMS - 1, 2, 64, LANES), F32),
             pltpu.VMEM((2, 64, LANES), F32),
@@ -543,7 +604,7 @@
             dma((2, 2)),
             dma((2, 2)),
             dma((2,)),
-            dma((2, 2)),
+            dma((2, 3)),
             dma((2, 2)),
             pltpu.SemaphoreType.REGULAR,
             pltpu.SemaphoreType.REGULAR,

time: 55.4 us -> 52.9 us (0.955)
  the two profiles are of different devices: /device:TPU:1 before, /device:TPU:17 now
where the time goes in v3:
time: 52.9 us; the launch traced here: 52.7 us
  Pallas kernels  51.1 us (97%)
  local copies, waits for them, and re-layouts  1.57 us (3%)
    pallas_call x1, Pallas kernels, per_device(): pl.pallas_call(kernel, out_shape=jax.ShapeDtypeStruct(control.shape, F32)...  51.1 us
    unnamed x1, local copies, waits for them, and re-layouts  1.57 us

profile of v3, /device:TPU:17, one launch (start us, length us, event | category | flops | bytes accessed | tf_op | source)
XLA Modules:
  0.0 52.7 jit_solution(15469993497108054019)
XLA Ops:
  0.0 51.1 %hybrid_gradient.1 = f32[2,2,32,256]{3,2,1,0:T(8,128)} custom-call(bf16[2,2,32,256]{3,2,1,0:T(8,128)(2,1)} %control_hbm.1, bf16[2,64,256]{2,1,0:T(8,128)(2,1)} %members_hbm.1, f32[2,32,256]{2,1,0:T(8,128)} %east_hbm.1, f32[2,32,256]{2,1,0:T(8,128)} %south_hbm.1, f32[64,256]{1,0:T(8,128)} %innovation_hbm.1, s32[64,256]{1,0:T(8,128)} %huber_hbm.1, ...), custom_call_target="tpu_custom_call" | custom-call | tf_op jit(solution)/shard_map/hybrid_gradient/pallas_call | solution.py:569
  51.1 1.6 %copy.10 = f32[2,2,32,256]{3,2,1,0:T(8,128)} copy(f32[2,2,32,256]{3,2,1,0:T(8,128)} %hybrid_gradient.1) | data formatting | bytes 262144

commit v4 on v3

--- a/solution.py
+++ b/solution.py
@@ -20,6 +20,7 @@
 WIDE = 8
 MEMS = 8
 ROOT = MEMS - 1
+DIRECT = 2
 BLOCKS = 4
 FAR_FIRST = (4, 3, 5, 2, 6, 1, 7, 0)
 
@@ -421,23 +422,24 @@
     def landing(side):
         return FIRST + LATS if side == 0 else 0
 
-    def direct_copy(side, column, row):
-        return remote(lift.at[tiles(column, 1), :], back_fields.at[0, tiles(landing(side) + across, 1), :],
-                      block_sems.at[side, 2], relay_sems.at[side, 1], lev=column, row=row)
+    def direct_copy(side, peer, row):
+        return remote(lift.at[tiles(peer, 1), :], back_fields.at[0, tiles(landing(side) + across, 1), :],
+                      block_sems.at[side, 2], relay_sems.at[side, 1], lev=peer, row=row)
 
     def send_edges(side, positions, row):
         for apart in FAR_FIRST:
-            direct_copy(side, lax.rem(across + apart, WIDE), row).start()
+            for position in range(DIRECT):
+                direct_copy(side, WIDE * position + lax.rem(across + apart, WIDE), row).start()
         for position in positions:
             block_copy(side, position, row).start()
 
     @pl.when(from_low == 1)
     def _():
-        send_edges(0, (1, 2, 3), r - 1)
+        send_edges(0, range(DIRECT, 4), r - 1)
 
     @pl.when(from_high == 1)
     def _():
-        send_edges(1, (3, 2, 1), r + 1)
+        send_edges(1, range(3, DIRECT - 1, -1), r + 1)
 
     for apart in FAR_FIRST:
         for turn in range(4):
@@ -462,11 +464,11 @@
                       back_fields.at[0, tiles(landing(side), count), :],
                       relay_sems.at[side, 0], relay_sems.at[side, 1], lev=l)
 
-    @pl.when((r > 0) & (along > 0))
+    @pl.when((r > 0) & (along >= DIRECT))
     def _():
         hand_on(1)
 
-    @pl.when((r < BLOCKS - 1) & (along > 0))
+    @pl.when((r < BLOCKS - 1) & (along >= DIRECT))
     def _():
         hand_on(0)
 
@@ -476,11 +478,11 @@
     diffuse_inside(back_fields, coefs)
 
     def halo_arrived(side):
-        @pl.when(along > 0)
+        @pl.when(along >= DIRECT)
         def _():
             handed(side, WIDE - 1).wait_recv()
 
-        @pl.when(along == 0)
+        @pl.when(along < DIRECT)
         def _():
             handed(side, WIDE).wait_recv()
 
@@ -511,7 +513,7 @@
         for copy in edge_copies(0, r - 1):
             copy.wait_send()
 
-        @pl.when(along > 0)
+        @pl.when(along >= DIRECT)
         def _():
             handed(1, WIDE - 1).wait_send()
 
@@ -520,7 +522,7 @@
         for copy in edge_copies(1, r + 1):
             copy.wait_send()
 
-        @pl.when(along > 0)
+        @pl.when(along >= DIRECT)
         def _():
             handed(0, WIDE - 1).wait_send()
 
@@ -543,7 +545,7 @@
         rest(1, share_sems).wait_send()
 
     def edges_sent(side):
-        for way, count in ((0, LEVS - WIDE), (2, WIDE)):
+        for way, count in ((0, LEVS - DIRECT * WIDE), (2, DIRECT * WIDE)):
             remote(lift.at[tiles(0, count), :], lift.at[tiles(0, count), :],
                    block_sems.at[side, way], block_sems.at[side, 1], lev=l).wait_send()
 

time: 52.9 us -> 51.8 us (0.979)
  the two profiles are of different devices: /device:TPU:17 before, /device:TPU:1 now
where the time goes in v4:
time: 51.8 us; the launch traced here: 51.3 us
  Pallas kernels  49.7 us (96%)
  local copies, waits for them, and re-layouts  1.57 us (3%)
    pallas_call x1, Pallas kernels, per_device(): pl.pallas_call(kernel, out_shape=jax.ShapeDtypeStruct(control.shape, F32)...  49.7 us
    unnamed x1, local copies, waits for them, and re-layouts  1.57 us

profile of v4, /device:TPU:1, one launch (start us, length us, event | category | flops | bytes accessed | tf_op | source)
XLA Modules:
  0.0 51.3 jit_solution(6871463172426938474)
XLA Ops:
  0.0 49.7 %hybrid_gradient.1 = f32[2,2,32,256]{3,2,1,0:T(8,128)} custom-call(bf16[2,2,32,256]{3,2,1,0:T(8,128)(2,1)} %control_hbm.1, bf16[2,64,256]{2,1,0:T(8,128)(2,1)} %members_hbm.1, f32[2,32,256]{2,1,0:T(8,128)} %east_hbm.1, f32[2,32,256]{2,1,0:T(8,128)} %south_hbm.1, f32[64,256]{1,0:T(8,128)} %innovation_hbm.1, s32[64,256]{1,0:T(8,128)} %huber_hbm.1, ...), custom_call_target="tpu_custom_call" | custom-call | tf_op jit(solution)/shard_map/hybrid_gradient/pallas_call | solution.py:571
  49.7 1.6 %copy.10 = f32[2,2,32,256]{3,2,1,0:T(8,128)} copy(f32[2,2,32,256]{3,2,1,0:T(8,128)} %hybrid_gradient.1) | data formatting | bytes 262144

commit v5 on v4

--- a/solution.py
+++ b/solution.py
@@ -132,8 +132,8 @@
 
 def kernel(
     control_hbm, members_hbm, east_hbm, south_hbm, innovation_hbm, huber_hbm, band_hbm, group_hbm,
-    out_hbm,
-    control, members, east_in, south_in, innovation, huber, band, group, out,
+    out,
+    control, members, east_in, south_in, innovation, huber, band, group,
     east, west, south, fields, back_fields, east_edge, south_edge,
     gathered, lift, relay, full_matrix, lower_matrix, upper_matrix,
     term, parts, share,
@@ -505,8 +505,6 @@
                 ]
                 out[member, level, :, lanes] = control[member, level, :, lanes].astype(F32) + smooth
 
-    store = pltpu.make_async_copy(out, out_hbm, local_sems.at[0])
-    store.start()
 
     @pl.when(r > 0)
     def _():
@@ -558,7 +556,6 @@
         edges_sent(1)
 
     columns.wait_send()
-    store.wait()
 
 
 def per_device(
@@ -572,7 +569,7 @@
         kernel,
         out_shape=jax.ShapeDtypeStruct(control.shape, F32),
         in_specs=[hbm] * 8,
-        out_specs=hbm,
+        out_specs=pl.BlockSpec(memory_space=pltpu.VMEM),
         scratch_shapes=[
             pltpu.VMEM(control.shape, jnp.bfloat16),
             pltpu.VMEM(members.shape, jnp.bfloat16),
@@ -582,7 +579,6 @@
             pltpu.VMEM(huber_class.shape, jnp.int32),
             pltpu.VMEM(band.shape, F32),
             pltpu.VMEM(group.shape, jnp.int32),
-            pltpu.VMEM(control.shape, F32),
             rows,
             rows,
             rows,
@@ -611,9 +607,9 @@
             pltpu.SemaphoreType.REGULAR,
             pltpu.SemaphoreType.REGULAR,
         ],
-        compiler_params=pltpu.CompilerParams(collective_id=0, has_side_effects=True),
+        compiler_params=pltpu.CompilerParams(collective_id=0, has_side_effects=True, vmem_limit_bytes=16 << 20),
         name="hybrid_gradient",
-    )(control, members, east_coef, south_coef, innovation, huber_class, band, group)
+    )(*[pltpu.with_memory_space_constraint(x, pltpu.HBM) for x in (control, members, east_coef, south_coef, innovation, huber_class, band, group)])
 
 
 def solution(mesh):

time: 51.8 us -> 50.3 us (0.971)
  local copies, waits for them, and re-layouts: 1.57 us -> 0.66 us
  Pallas kernels: 49.7 us -> 49.1 us
    unnamed x1, local copies, waits for them, and re-layouts: 1.57 us -> 0.66 us
    pallas_call x1, Pallas kernels: 49.7 us -> 49.1 us  [per_device(): pl.pallas_call(kernel, out_shape=jax.ShapeDtypeStruct(control.shape, F32)...]
where the time goes in v5:
time: 50.3 us; the launch traced here: 49.8 us
  Pallas kernels  49.1 us (98%)
  local copies, waits for them, and re-layouts  0.66 us (1%)
    pallas_call x1, Pallas kernels, per_device(): pl.pallas_call(kernel, out_shape=jax.ShapeDtypeStruct(control.shape, F32)...  49.1 us

profile of v5, /device:TPU:1, one launch (start us, length us, event | category | flops | bytes accessed | tf_op | source)
XLA Modules:
  0.0 49.8 jit_solution(10633781566401412951)
XLA Ops:
  0.0 49.1 %hybrid_gradient.1 = f32[2,2,32,256]{3,2,1,0:T(8,128)S(1)} custom-call(bf16[2,2,32,256]{3,2,1,0:T(8,128)(2,1)} %control_hbm.1, bf16[2,64,256]{2,1,0:T(8,128)(2,1)} %members_hbm.1, f32[2,32,256]{2,1,0:T(8,128)} %east_hbm.1, f32[2,32,256]{2,1,0:T(8,128)} %south_hbm.1, f32[64,256]{1,0:T(8,128)} %innovation_hbm.1, s32[64,256]{1,0:T(8,128)} %huber_hbm.1, ...), custom_call_target="tpu_custom_call" | custom-call | tf_op jit(solution)/shard_map/hybrid_gradient/pallas_call | solution.py:568
  49.1 0.7 %copy.10 = f32[2,2,32,256]{3,2,1,0:T(8,128)} copy(f32[2,2,32,256]{3,2,1,0:T(8,128)S(1)} %hybrid_gradient.1) | data formatting | bytes 262144

commit v6 on v5

--- a/solution.py
+++ b/solution.py
@@ -20,7 +20,7 @@
 WIDE = 8
 MEMS = 8
 ROOT = MEMS - 1
-DIRECT = 2
+DIRECT = 1
 BLOCKS = 4
 FAR_FIRST = (4, 3, 5, 2, 6, 1, 7, 0)
 
@@ -138,7 +138,7 @@
     gathered, lift, relay, full_matrix, lower_matrix, upper_matrix,
     term, parts, share,
     local_sems, edge_send, edge_recv, fwd_sems, sum_sems, share_sems,
-    back_sems, block_sems, relay_sems, lev_ready, mem_ready,
+    back_sems, block_sems, relay_sems, pair_sems, lev_ready, mem_ready,
 ):
     m, l, r = lax.axis_index("mem"), lax.axis_index("lev"), lax.axis_index("row")
     along, across = l // WIDE, lax.rem(l, WIDE)
@@ -148,6 +148,9 @@
     high_edge = (l + HALO) // LEVS
     from_low = low_edge * has_lower
     from_high = high_edge * has_upper
+    parity = lax.rem(r, 2)
+    pair_along = 3 * (1 - parity)
+    in_pair_rows = jnp.where(along == pair_along, 1, 0)
     coefs = (east, west, south)
 
     def leader(row):
@@ -339,7 +342,7 @@
 
     keep_lower = has_lower.astype(F32)
     diffuse_edges(fields, coefs, keep_lower)
-    send_latitudes((0, 3))
+    send_latitudes((3, 0))
 
     gathered[tiles(l, 1), :] = fields[PASSES, tiles(FIRST + l, 1), :]
     everyone = remote(fields.at[PASSES, tiles(FIRST, LEVS - 1), :], gathered.at[tiles(0, LEVS - 1), :],
@@ -427,26 +430,26 @@
                       block_sems.at[side, 2], relay_sems.at[side, 1], lev=peer, row=row)
 
     def send_edges(side, positions, row):
-        for apart in FAR_FIRST:
-            for position in range(DIRECT):
+        for position in range(DIRECT):
+            for apart in FAR_FIRST:
                 direct_copy(side, WIDE * position + lax.rem(across + apart, WIDE), row).start()
         for position in positions:
             block_copy(side, position, row).start()
 
-    @pl.when(from_low == 1)
-    def _():
-        send_edges(0, range(DIRECT, 4), r - 1)
-
-    @pl.when(from_high == 1)
-    def _():
-        send_edges(1, range(3, DIRECT - 1, -1), r + 1)
+    @pl.when((r == 2) & (low_edge == 1))
+    def _():
+        send_edges(0, range(DIRECT, 4), 1)
+
+    @pl.when((r == 1) & (high_edge == 1))
+    def _():
+        send_edges(1, range(3, DIRECT - 1, -1), 2)
 
     for apart in FAR_FIRST:
         for turn in range(4):
             if apart or turn:
                 peer = WIDE * lax.rem(along + turn, 4) + lax.rem(across + apart, WIDE)
                 remote(lift.at[tiles(peer, 1), :], back_fields.at[0, tiles(FIRST + l, 1), :],
-                       back_sems.at[0], back_sems.at[1], lev=peer).start()
+                       back_sems.at[0], back_sems.at[2 - in_pair_rows], lev=peer).start()
 
     back_fields[0, tiles(FIRST + l, 1), :] = lift[tiles(l, 1), :]
 
@@ -464,18 +467,60 @@
                       back_fields.at[0, tiles(landing(side), count), :],
                       relay_sems.at[side, 0], relay_sems.at[side, 1], lev=l)
 
-    @pl.when((r > 0) & (along >= DIRECT))
+    @pl.when((r == 2) & (along >= DIRECT))
     def _():
         hand_on(1)
 
-    @pl.when((r < BLOCKS - 1) & (along >= DIRECT))
+    @pl.when((r == 1) & (along >= DIRECT))
     def _():
         hand_on(0)
 
-    columns = remote(lift.at[tiles(0, LEVS - 1), :], back_fields.at[0, tiles(FIRST, LEVS - 1), :],
-                     back_sems.at[0], back_sems.at[1], lev=l)
-    columns.wait_recv()
+    def columns(group, count):
+        return remote(lift.at[tiles(0, count), :], back_fields.at[0, tiles(FIRST, count), :],
+                      back_sems.at[0], back_sems.at[group], lev=l)
+
+    def to_pair(source, target, row):
+        return remote(back_fields.at[0, tiles(source, HALO), :], back_fields.at[0, tiles(target, HALO), :],
+                      pair_sems.at[0], pair_sems.at[1], row=row)
+
+    def pair_copy(even, row):
+        if even:
+            return to_pair(FIRST + LATS - HALO, 0, row)
+        return to_pair(FIRST, FIRST + LATS, row)
+
+    @pl.when(in_pair_rows == 1)
+    def _():
+        columns(1, WIDE - 1).wait_recv()
+
+    @pl.when(in_pair_rows == 0)
+    def _():
+        columns(1, WIDE).wait_recv()
+
+    @pl.when(parity == 0)
+    def _():
+        pair_copy(True, r + 1).start()
+
+    @pl.when(parity == 1)
+    def _():
+        pair_copy(False, r - 1).start()
+
+    @pl.when(in_pair_rows == 1)
+    def _():
+        columns(2, LEVS - WIDE).wait_recv()
+
+    @pl.when(in_pair_rows == 0)
+    def _():
+        columns(2, LEVS - WIDE - 1).wait_recv()
+
     diffuse_inside(back_fields, coefs)
+
+    @pl.when(parity == 0)
+    def _():
+        pair_copy(False, r + 1).wait_recv()
+
+    @pl.when(parity == 1)
+    def _():
+        pair_copy(True, r - 1).wait_recv()
 
     def halo_arrived(side):
         @pl.when(along >= DIRECT)
@@ -486,11 +531,11 @@
         def _():
             handed(side, WIDE).wait_recv()
 
-    @pl.when(r > 0)
+    @pl.when(r == 2)
     def _():
         halo_arrived(1)
 
-    @pl.when(r < BLOCKS - 1)
+    @pl.when(r == 1)
     def _():
         halo_arrived(0)
 
@@ -511,18 +556,26 @@
         for copy in edge_copies(0, r - 1):
             copy.wait_send()
 
-        @pl.when(along >= DIRECT)
-        def _():
-            handed(1, WIDE - 1).wait_send()
-
     @pl.when(r < BLOCKS - 1)
     def _():
         for copy in edge_copies(1, r + 1):
             copy.wait_send()
 
-        @pl.when(along >= DIRECT)
-        def _():
-            handed(0, WIDE - 1).wait_send()
+    @pl.when((r == 2) & (along >= DIRECT))
+    def _():
+        handed(1, WIDE - 1).wait_send()
+
+    @pl.when((r == 1) & (along >= DIRECT))
+    def _():
+        handed(0, WIDE - 1).wait_send()
+
+    @pl.when(parity == 0)
+    def _():
+        pair_copy(True, r + 1).wait_send()
+
+    @pl.when(parity == 1)
+    def _():
+        pair_copy(False, r - 1).wait_send()
 
     everyone.wait_send()
 
@@ -547,15 +600,15 @@
             remote(lift.at[tiles(0, count), :], lift.at[tiles(0, count), :],
                    block_sems.at[side, way], block_sems.at[side, 1], lev=l).wait_send()
 
-    @pl.when(from_low == 1)
+    @pl.when((r == 2) & (low_edge == 1))
     def _():
         edges_sent(0)
 
-    @pl.when(from_high == 1)
+    @pl.when((r == 1) & (high_edge == 1))
     def _():
         edges_sent(1)
 
-    columns.wait_send()
+    columns(1, LEVS - 1).wait_send()
 
 
 def per_device(
@@ -601,9 +654,10 @@
             dma((2,)),
             dma((2, 2)),
             dma((2, 2)),
-            dma((2,)),
+            dma((3,)),
             dma((2, 3)),
             dma((2, 2)),
+            dma((2,)),
             pltpu.SemaphoreType.REGULAR,
             pltpu.SemaphoreType.REGULAR,
         ],

time: 50.3 us -> 50 us (level)
  no operation moved by 1% of the time
where the time goes in v6:
time: 50 us; the launch traced here: 49.9 us
  Pallas kernels  49.2 us (98%)
  local copies, waits for them, and re-layouts  0.66 us (1%)
    pallas_call x1, Pallas kernels, per_device(): pl.pallas_call(kernel, out_shape=jax.ShapeDtypeStruct(control.shape, F32)...  49.2 us

profile of v6, /device:TPU:1, one launch (start us, length us, event | category | flops | bytes accessed | tf_op | source)
XLA Modules:
  0.0 49.9 jit_solution(14850055121707443793)
XLA Ops:
  0.0 49.2 %hybrid_gradient.1 = f32[2,2,32,256]{3,2,1,0:T(8,128)S(1)} custom-call(bf16[2,2,32,256]{3,2,1,0:T(8,128)(2,1)} %control_hbm.1, bf16[2,64,256]{2,1,0:T(8,128)(2,1)} %members_hbm.1, f32[2,32,256]{2,1,0:T(8,128)} %east_hbm.1, f32[2,32,256]{2,1,0:T(8,128)} %south_hbm.1, f32[64,256]{1,0:T(8,128)} %innovation_hbm.1, s32[64,256]{1,0:T(8,128)} %huber_hbm.1, ...), custom_call_target="tpu_custom_call" | custom-call | tf_op jit(solution)/shard_map/hybrid_gradient/pallas_call | solution.py:621
  49.2 0.7 %copy.10 = f32[2,2,32,256]{3,2,1,0:T(8,128)} copy(f32[2,2,32,256]{3,2,1,0:T(8,128)S(1)} %hybrid_gradient.1) | data formatting | bytes 262144

commit v7 on v6

--- a/solution.py
+++ b/solution.py
@@ -300,29 +300,29 @@
         set_west(first)
     diffuse_inside(fields, coefs)
 
-    pl.semaphore_wait(lev_ready, 1 - is_leader + from_low + from_high)
-
-    def send_latitudes(rows):
-        for apart in FAR_FIRST:
-            for row in rows:
-                peer = WIDE * row + lax.rem(across + apart, WIDE)
-
-                def send(peer=peer):
-                    remote(fields.at[PASSES, tiles(FIRST + peer, 1), :], gathered.at[tiles(l, 1), :],
-                           fwd_sems.at[0], fwd_sems.at[1], lev=peer).start()
-
-                if apart:
-                    send()
-                else:
-                    pl.when(along != row)(send)
-
-    send_latitudes((1, 2))
-
     for load in loads[3:]:
         load.wait()
     vertical_columns(band, group, full_matrix)
     split_matrix(full_matrix[...], upper_matrix)
     split_matrix(full_matrix[...].T, lower_matrix)
+
+    pl.semaphore_wait(lev_ready, 1 - is_leader + from_low + from_high)
+
+    def send_latitudes(rows):
+        for apart in FAR_FIRST:
+            for row in rows:
+                peer = WIDE * row + lax.rem(across + apart, WIDE)
+
+                def send(peer=peer):
+                    remote(fields.at[PASSES, tiles(FIRST + peer, 1), :], gathered.at[tiles(l, 1), :],
+                           fwd_sems.at[0], fwd_sems.at[1], lev=peer).start()
+
+                if apart:
+                    send()
+                else:
+                    pl.when(along != row)(send)
+
+    send_latitudes((1, 2))
 
     def take_edge(side, first):
         for copy in edge_copies(side, r):

time: 50 us -> 49.8 us (level)
  no operation moved by 1% of the time
where the time goes in v7:
time: 49.8 us; the launch traced here: 49.6 us
  Pallas kernels  49 us (98%)
  local copies, waits for them, and re-layouts  0.66 us (1%)
    pallas_call x1, Pallas kernels, per_device(): pl.pallas_call(kernel, out_shape=jax.ShapeDtypeStruct(control.shape, F32)...  49 us

profile of v7, /device:TPU:1, one launch (start us, length us, event | category | flops | bytes accessed | tf_op | source)
XLA Modules:
  0.0 49.6 jit_solution(18041528904611836885)
XLA Ops:
  0.0 49.0 %hybrid_gradient.1 = f32[2,2,32,256]{3,2,1,0:T(8,128)S(1)} custom-call(bf16[2,2,32,256]{3,2,1,0:T(8,128)(2,1)} %control_hbm.1, bf16[2,64,256]{2,1,0:T(8,128)(2,1)} %members_hbm.1, f32[2,32,256]{2,1,0:T(8,128)} %east_hbm.1, f32[2,32,256]{2,1,0:T(8,128)} %south_hbm.1, f32[64,256]{1,0:T(8,128)} %innovation_hbm.1, s32[64,256]{1,0:T(8,128)} %huber_hbm.1, ...), custom_call_target="tpu_custom_call" | custom-call | tf_op jit(solution)/shard_map/hybrid_gradient/pallas_call | solution.py:621
  49.0 0.7 %copy.10 = f32[2,2,32,256]{3,2,1,0:T(8,128)} copy(f32[2,2,32,256]{3,2,1,0:T(8,128)S(1)} %hybrid_gradient.1) | data formatting | bytes 262144
